TPU v7x, 32 devices: a whole 2x2x4 slice. The times are simulated.
32 devices in a mesh: prow: 8 (over y, x, core), pcol: 4 (over z).
Axes of the slice: x: 2, y: 2, z: 4, core: 2. Of those that a mesh axis runs over, the one named last changes fastest.
Arguments:
- matrix: float32 [4096, 4096], P('prow', 'pcol'), may hold values from -6 to 6
- pivots: int32 [2, 512], replicated, may hold values from 0 to 4095, as said below
- lower_inv: float32 [2, 512, 512], replicated, as said below
- upper_inv: float32 [2, 512, 512], replicated, as said below
Outputs:
- factored: float32 [4096, 4096], P('prow', 'pcol')
Inputs may be any that keep to these rules, and one draw needn't show every extreme that they name: The entries of pivots[k] are distinct row indices from k * 512 to 4095. Each lower_inv[k] is lower triangular. Each upper_inv[k] is upper triangular.
All inputs are finite; a program needn't handle non-finite values.
Results may differ from a plain program's by a relative error of at most 0.0001.
Values sent between devices are 32-bit elements; how exact they have to be, the bound alone decides.
No kernel may reach another device: no remote copies, remote signals or barrier semaphores. Data moves between devices by JAX's collectives and lax.ppermute only.
A program may use at most 128 MiB of HBM per device.

v0:
```python
import jax
import jax.numpy as jnp
from jax import lax
from jax.experimental import pallas as pl
from jax.experimental.pallas import tpu as pltpu
from jax.sharding import PartitionSpec as P

BATCH = 320
SHARE = 80
F32, BF16 = jnp.float32, jnp.bfloat16
SMEM, VMEM, ANY = (pl.BlockSpec(memory_space=space) for space in (pltpu.SMEM, pltpu.VMEM, pl.ANY))
PARAMS = pltpu.CompilerParams(vmem_limit_bytes=56 << 20)


def split(x):
    high = x.astype(BF16)
    return high, (x - high.astype(F32)).astype(BF16)


def mul(left, right):
    dot = lambda a, b: jnp.dot(a, b, preferred_element_type=F32)
    return dot(left[0], right[0]) + (dot(left[0], right[1]) + dot(left[1], right[0]))


def product(left, right):
    return jnp.dot(left, right, precision=lax.Precision.HIGH, preferred_element_type=F32)


def displaced(pivot_row, start_row):
    width = pivot_row.shape[0]
    end_row = start_row + width
    window = start_row + jnp.arange(width, dtype=jnp.int32)
    chosen = jnp.any(pivot_row[None, :] == window[:, None], axis=1)
    unnamed = jnp.logical_not(chosen)
    free_rank = jnp.cumsum(unnamed.astype(jnp.int32)) - 1
    outside = pivot_row >= end_row
    out_rank = jnp.sum(
        (outside[None, :] & (pivot_row[None, :] < pivot_row[:, None])).astype(jnp.int32), axis=1
    )
    matches = unnamed[None, :] & (free_rank[None, :] == out_rank[:, None])
    source = jnp.sum(jnp.where(matches, window[None, :], 0), axis=1)
    return (source, outside)


def pick(own, mate, lists, pieces, shape):
    rows, cols = own.shape
    count = len(lists)

    def body(*refs):
        index_refs, (own_ref, mate_ref, out_ref, chip, sems) = refs[:count], refs[count:]
        copies = [
            pltpu.make_async_copy(own_ref, chip.at[pl.ds(0, rows)], sems.at[0]),
            pltpu.make_async_copy(mate_ref, chip.at[pl.ds(rows, rows)], sems.at[1]),
        ]
        for copy in copies:
            copy.start()
        for copy in copies:
            copy.wait()
        for number, source, row, column, width in pieces:

            def step(i, carry):
                wanted = index_refs[number][i]
                value = chip[pl.ds(jnp.maximum(wanted, 0), 1), source : source + width]
                out_ref[pl.ds(row + i, 1), column : column + width] = jnp.where(wanted >= 0, value, 0.0)
                return carry

            lax.fori_loop(0, lists[number].shape[0], step, 0, unroll=8)

    return pl.pallas_call(
        body,
        out_shape=jax.ShapeDtypeStruct(shape, F32),
        in_specs=[SMEM] * count + [ANY, ANY],
        out_specs=VMEM,
        scratch_shapes=[pltpu.VMEM((2 * rows, cols), F32), pltpu.SemaphoreType.DMA((2,))],
        compiler_params=PARAMS,
        name="pick",
    )(*lists, own, mate)


def middle_step(matrix, one, mine, mate, lower, upper_one, upper_two, core, slots, targets, count, size):
    rows, cols = matrix.shape
    width = lower.shape[0]
    half = width // 2
    blocks = cols // width
    part = (rows + SHARE) // 2

    def body(core_ref, slot_ref, target_ref, count_ref, matrix_ref, one_ref, mine_ref, mate_ref, lower_ref, u1_ref, u2_ref,
             block_ref, upper_ref, under_ref, panel_ref, raw, pair, new_one):
        block_ref[...] = matrix_ref[...]
        raw[...] = jnp.zeros_like(raw)

        def bring(i, carry):
            slot, row = slot_ref[i], target_ref[i]
            here = slot < size
            at = half + jnp.where(here, slot, slot - size)
            for b in range(blocks):
                value = jnp.where(here, mine_ref[pl.ds(at + b * size, 1), :], mate_ref[pl.ds(at + b * size, 1), :])
                block_ref[pl.ds(row, 1), b * width : (b + 1) * width] = value
                if b == 0:
                    raw[pl.ds(i, 1), :] = value
            return carry

        lax.fori_loop(0, count_ref[0], bring, 0)
        fresh = mul(split(raw[...]), split(u1_ref[...]))
        pair[pl.ds(rows, SHARE), :] = fresh
        new_one[...] = one_ref[...]

        def renew(i, carry):
            new_one[pl.ds(target_ref[i], 1), :] = pair[pl.ds(rows + i, 1), :]
            return carry

        lax.fori_loop(0, count_ref[0], renew, 0)
        first = pl.multiple_of(core_ref[0] * half, half)
        second = pl.multiple_of(half - core_ref[0] * half, half)
        panel = mul(split(lower_ref[:, pl.ds(first, half)]), split(mine_ref[:half, :])) + mul(
            split(lower_ref[:, pl.ds(second, half)]), split(mate_ref[:half, :])
        )
        panel_ref[...] = panel
        rest = block_ref[:, width : 2 * width] - mul(split(new_one[...]), split(panel))
        pair[pl.ds(0, rows), :] = mul(split(rest), split(u2_ref[...]))
        upper_ref[...] = pair[:part, :]
        under_ref[...] = pair[part:, :]

    shape = lambda *s: jax.ShapeDtypeStruct(s, F32)
    return pl.pallas_call(
        body,
        out_shape=(shape(rows, cols), shape(part, width), shape(part, width), shape(width, width)),
        in_specs=[SMEM] * 4 + [VMEM] * 7,
        out_specs=(VMEM,) * 4,
        scratch_shapes=[pltpu.VMEM(s, F32) for s in ((SHARE, width), (rows + SHARE, width), (rows, width))],
        compiler_params=PARAMS,
        name="middle",
    )(core, slots, targets, count, matrix, one, mine, mate, lower, upper_one, upper_two)


def row_step(where, panel, mine, mate, top_mine, top_mate, lower, cols):
    width = panel.shape[0]
    half = width // 2
    blocks = cols // width
    offset = cols - width

    def body(where_ref, panel_ref, mine_ref, mate_ref, tm_ref, tt_ref, lower_ref, high_ref, low_ref, edge_ref, second):
        me, first_column = where_ref[0], where_ref[1] == 0
        core = me % 2
        first = pl.multiple_of(core * half, half)
        other = pl.multiple_of(half - core * half, half)
        lower = lambda k: (split(lower_ref[k, :, pl.ds(first, half)]), split(lower_ref[k, :, pl.ds(other, half)]))
        one, two = lower(0), lower(1)
        tops = (split(tm_ref[...]), split(tt_ref[...]))
        for b in range(blocks):
            at = slice(b * width, (b + 1) * width)
            source = slice((b if b < 1 else b - 1) * width, ((b if b < 1 else b - 1) + 1) * width)
            if b == 1:
                row_one = panel_ref[...]
            else:
                row_one = mul(one[0], split(mine_ref[:, source])) + mul(one[1], split(mate_ref[:, source]))
            kept = jnp.where(first_column, 0.0, row_one) if b < 1 else row_one
            pair = split(kept)
            high_ref[:width, at], low_ref[:width, at] = pair
            rest = slice(offset + b * width, offset + (b + 1) * width)
            second[:half, :] = mine_ref[:, rest] - mul(tops[0], pair)
            second[half:, :] = mate_ref[:, rest] - mul(tops[1], pair)
            row_two = mul(two[0], split(second[:half, :])) + mul(two[1], split(second[half:, :]))
            kept = jnp.where(first_column, 0.0, row_two) if b < 2 else row_two
            high_ref[width:, at], low_ref[width:, at] = split(kept)

            @pl.when(me == 0)
            def _():
                if b >= 1:
                    edge_ref[:, at] = row_one
                else:
                    edge_ref[:half, at] = jnp.where(first_column, mine_ref[:, source], row_one[:half, :])
                    edge_ref[half:, at] = jnp.where(first_column, mate_ref[:, source], row_one[half:, :])

            @pl.when(me != 0)
            def _():
                if b >= 2:
                    edge_ref[:, at] = row_two
                elif b == 1:
                    edge_ref[:half, at] = jnp.where(first_column, second[half:, :], row_two[:half, :])
                    edge_ref[half:, at] = jnp.where(first_column, second[:half, :], row_two[half:, :])
                else:
                    edge_ref[:half, at] = jnp.where(first_column, tt_ref[...], row_two[:half, :])
                    edge_ref[half:, at] = jnp.where(first_column, tm_ref[...], row_two[half:, :])

    return pl.pallas_call(
        body,
        out_shape=(
            jax.ShapeDtypeStruct((2 * width, cols), BF16),
            jax.ShapeDtypeStruct((2 * width, cols), BF16),
            jax.ShapeDtypeStruct((width, cols), F32),
        ),
        in_specs=[SMEM] + [VMEM] * 6,
        out_specs=(VMEM,) * 3,
        scratch_shapes=[pltpu.VMEM((width, width), F32)],
        compiler_params=PARAMS,
        name="rows",
    )(where, panel, mine, mate, top_mine, top_mate, lower)


def finish_step(where, targets, count, block, ones, uppers, unders, high, low, edge, held):
    rows, cols = block.shape
    width = ones[0].shape[1]
    part = uppers[0].shape[0]
    parts = len(ones)
    chunk = min(rows, 128)

    def body(*refs):
        where_ref, target_ref, count_ref, block_ref, high_ref, low_ref = refs[:6]
        one_refs, upper_refs, under_refs = (refs[6 + parts * k : 6 + parts * (k + 1)] for k in range(3))
        edge_ref, out_ref, one, pair, sems = refs[6 + 3 * parts :]
        me, column = where_ref[0], where_ref[1]
        first_column = column == 0
        for k in range(parts):
            mine = column == held[k][0]
            for z in held[k][1:]:
                mine = mine | (column == z)

            @pl.when((me >= 2) & mine)
            def _():
                copies = [
                    pltpu.make_async_copy(one_refs[k], one, sems.at[0]),
                    pltpu.make_async_copy(upper_refs[k], pair.at[pl.ds(0, part)], sems.at[1]),
                    pltpu.make_async_copy(under_refs[k], pair.at[pl.ds(part, part)], sems.at[2]),
                ]
                for copy in copies:
                    copy.start()
                for copy in copies:
                    copy.wait()

        @pl.when(me < 2)
        def _():
            copy = pltpu.make_async_copy(edge_ref, out_ref, sems.at[0])
            copy.start()
            copy.wait()

        @pl.when(me >= 2)
        def _():
            def renew(i, carry):
                one[pl.ds(target_ref[i], 1), :] = pair[pl.ds(rows + i, 1), :]
                return carry

            lax.fori_loop(0, count_ref[0], renew, 0)

            @pl.loop(0, rows // chunk)
            def _(c):
                at = pl.ds(pl.multiple_of(c * chunk, chunk), chunk)
                left = jnp.concatenate([one[at, :], pair[at, :]], axis=1)
                total = block_ref[at, :] - mul(split(left), (high_ref[...], low_ref[...]))
                out_ref[at, : 2 * width] = jnp.where(first_column, left, total[:, : 2 * width])
                if cols > 2 * width:
                    out_ref[at, 2 * width :] = total[:, 2 * width :]

    return pl.pallas_call(
        body,
        out_shape=jax.ShapeDtypeStruct((rows, cols), F32),
        in_specs=[SMEM] * 3 + [VMEM] * 3 + [ANY] * (3 * parts + 1),
        out_specs=VMEM,
        scratch_shapes=[
            pltpu.VMEM((rows, width), F32),
            pltpu.VMEM((rows + SHARE, width), F32),
            pltpu.SemaphoreType.DMA((3,)),
        ],
        compiler_params=PARAMS,
        name="finish",
    )(where, targets, count, block, high, low, *ones, *uppers, *unders, edge)


def place(target, rows, where_to, count):
    def body(where_ref, count_ref, target_ref, rows_ref, out_ref):
        out_ref[...] = target_ref[...]

        def step(i, carry):
            out_ref[pl.ds(where_ref[i], 1), :] = rows_ref[pl.ds(i, 1), :]
            return carry

        lax.fori_loop(0, count_ref[0], step, 0)

    return pl.pallas_call(
        body,
        out_shape=jax.ShapeDtypeStruct(target.shape, target.dtype),
        in_specs=[SMEM, SMEM, VMEM, VMEM],
        out_specs=VMEM,
        compiler_params=PARAMS,
        name="place",
    )(where_to, count, target, rows)


def swap_cores(x):
    return lax.ppermute(x, "prow", [(i, i ^ 1) for i in range(lax.axis_size("prow"))])


def gather_sum(x):
    devices = lax.axis_size("prow")
    bits = [1 << k for k in range(1, devices.bit_length() - 1)]
    turned = bits[len(bits) // 2 :] + bits[: len(bits) // 2]
    for first, second in zip(bits, turned):
        x = x + lax.ppermute(x, "prow", [(i, i ^ (second if i % 2 else first)) for i in range(devices)])
    return x, swap_cores(x)


def relay(x):
    count = lax.axis_size("pcol")
    parts = [x]
    for even in range(2, count, 2):
        current = lax.ppermute(x if even == 2 else parts[-2 if even > 4 else 1], "pcol", [(even - 2, even)])
        parts += [current, lax.ppermute(current, "pcol", [(even, even - 1)])]
        if even + 2 >= count and even + 1 < count:
            parts.append(lax.ppermute(current, "pcol", [(even, even + 1)]))
    return parts


def held_by(count):
    held = [[0]]
    for even in range(2, count, 2):
        held += [[even], [even - 1]]
        if even + 2 >= count and even + 1 < count:
            held.append([even + 1])
    return held


def joined(parts):
    total = parts[1]
    for part in parts[2:]:
        total = total + part
    return jnp.where(lax.axis_index("pcol") == 0, parts[0], total)


def shards(matrix, pivots, lower_inv, upper_inv):
    rows, cols = matrix.shape
    width = lower_inv.shape[1]
    devices = lax.axis_size("prow")
    if rows != width or cols < 2 * width or cols % width or pivots.shape[0] != 2 or devices < 4:
        raise ValueError("unsupported shapes")
    me, column = lax.axis_index("prow"), lax.axis_index("pcol")
    core = me % 2
    first_column = column == 0
    half = width // 2
    blocks = cols // width
    mate = swap_cores(matrix)

    column_one = product(matrix[:, :width], upper_inv[0])
    ones = relay(column_one)

    named, taken = pivots[0], pivots[1]
    source_one, outside_one = displaced(named, 0)
    source_two, outside_two = displaced(taken, width)
    same = taken[:, None] == named[None, :]
    again = source_two[:, None] == named[None, :]

    def origin(hit, position):
        return jnp.where(
            jnp.any(hit, axis=1), jnp.sum(jnp.where(hit, source_one[None, :], 0), axis=1), position
        )

    second_rows = origin(same, taken)
    valid = jnp.concatenate(
        [(named >= 2 * width) & jnp.logical_not(jnp.any(same, axis=0)), outside_two]
    )
    target = jnp.concatenate([named, taken])
    origin_row = jnp.concatenate([source_one, origin(again, source_two)])
    rank = jnp.cumsum(valid.astype(jnp.int32)) - 1
    moved = jnp.sum(valid.astype(jnp.int32))
    shares = jnp.sum(
        (valid[None, :] & ((target // rows)[None, :] == jnp.arange(devices, dtype=jnp.int32)[:, None])).astype(
            jnp.int32
        ),
        axis=1,
    )

    def ours(vector):
        size = vector.shape[0] // 2
        wanted = jnp.where(core == 0, vector[:size], vector[size:])
        mine, theirs = wanted - me * rows, wanted - (me + 1 - 2 * core) * rows
        inside = lambda v: (v >= 0) & (v < rows)
        return jnp.where(inside(mine), mine, jnp.where(inside(theirs), rows + theirs, -1))

    def batch(start, size):
        slots = start + jnp.arange(size, dtype=jnp.int32)
        chosen = valid[None, :] & (rank[None, :] == slots[:, None])
        origins = jnp.sum(jnp.where(chosen, origin_row[None, :], 0), axis=1)
        own = valid & (rank >= start) & (rank < start + size) & (target // rows == me)
        own_rank = jnp.cumsum(own.astype(jnp.int32)) - 1
        chosen = own[None, :] & (own_rank[None, :] == jnp.arange(SHARE, dtype=jnp.int32)[:, None])
        slot = (rank - start + core * (size // 2)) % size
        own_slot = jnp.sum(jnp.where(chosen, slot[None, :], 0), axis=1)
        own_row = jnp.sum(jnp.where(chosen, (target - me * rows)[None, :], 0), axis=1)
        count = jnp.minimum(jnp.sum(own.astype(jnp.int32)), SHARE)
        return ours(origins), own_slot, own_row, count[None]

    origins, own_slot, own_row, count = batch(0, BATCH)
    size = BATCH // 2
    lists = [ours(named), origins]
    pieces = [(0, width, 0, 0, width)] + [(1, b * width, half + b * size, 0, width) for b in range(blocks)]
    mine, mates = gather_sum(pick(matrix, mate, lists, pieces, (half + blocks * size, width)))
    block, upper, under, panel = middle_step(
        matrix, column_one, mine, mates, lower_inv[0], upper_inv[0], upper_inv[1], core[None], own_slot, own_row, count, size
    )
    uppers, unders = relay(upper), relay(under)

    lists = [ours(named), ours(second_rows)]
    pieces = [(0, 0, 0, 0, width)] + [(0, b * width, 0, (b - 1) * width, width) for b in range(2, blocks)]
    pieces += [(1, 0, 0, cols - width, cols)]
    mine, mates = gather_sum(pick(matrix, mate, lists, pieces, (half, 2 * cols - width)))

    one = joined(ones)
    top_mine, top_mate = gather_sum(pick(one, swap_cores(one), [ours(second_rows)], [(0, 0, 0, 0, width)], (half, width)))
    where = jnp.stack([me, column]).astype(jnp.int32)
    high, low, edge = row_step(where, panel, mine, mates, top_mine, top_mate, lower_inv, cols)
    held = held_by(lax.axis_size("pcol"))
    result = finish_step(where, own_row, count, block, ones, uppers, unders, high, low, edge, held)

    crowded = (moved > BATCH) | (jnp.max(shares) > SHARE)
    trips = jnp.where(crowded, (moved + SHARE - 1) // SHARE, 0)

    def more(number, result):
        origins, own_slot, own_row, count = batch(number * SHARE, SHARE)
        rows_here = gather_sum(pick(matrix, mate, [origins], [(0, 0, 0, 0, cols)], (SHARE // 2, cols)))
        raw = jnp.take(jnp.concatenate(rows_here, axis=0), own_slot, axis=0)
        one = product(raw[:, :width], upper_inv[0])
        two = product(raw[:, width : 2 * width] - product(one, panel), upper_inv[1])
        pair = joined(relay(jnp.concatenate([one, two], axis=1)))
        panels = high.astype(F32) + low.astype(F32)
        updated = raw - product(pair, panels)
        updated = jnp.concatenate(
            [jnp.where(first_column, pair, updated[:, : 2 * width]), updated[:, 2 * width :]], axis=1
        )
        return place(result, updated, own_row, count)

    return lax.fori_loop(0, trips, more, result)


def solution(mesh):
    in_specs = (P("prow", "pcol"), P(), P(), P())
    out_specs = P("prow", "pcol")
    return jax.shard_map(shards, mesh=mesh, in_specs=in_specs, out_specs=out_specs, check_vma=False)
```

profile of v0, /device:TPU:23, one launch (start us, length us, event | category | flops | bytes accessed | tf_op | source)
XLA Modules:
  0.0 193.5 jit_solution(10055181083963920016)
XLA Ops:
  0.0 0.7 collective-permute-start.6
  0.7 2.5 %fusion.39.one_ref.refs_6_ = f32[512,512]{1,0:T(8,128)S(1)} fusion(f32[512,1024]{1,0:T(8,128)} %refs_2_.3, f32[2,512,512]{2,1,0:T(8,128)} %param.9), kind=kOutput, calls=%fused_computation.88 | convolution fusion | flops 805306368 | bytes 3145728 | tf_op jit(solution)/shard_map/dot_general | solution.py:26
  3.2 1.3 collective-permute-start.13
  9.4 0.6 and_select_fusion.6.refs_1_
  10.1 0.6 and_select_fusion.7.refs_0_
  10.6 20.1 %collective-permute-done.13.refs_7_ = f32[512,512]{1,0:T(8,128)} collective-permute-done((f32[512,512]{1,0:T(8,128)S(1)}, f32[512,512]{1,0:T(8,128)}, u32[]{:S(2)}, u32[]{:S(2)}) %collective-permute-start.13) | collective-permute-done | bytes 1048608 | tf_op jit(solution)/shard_map/ppermute | solution.py:306
  30.7 2.3 %collective-permute-start.14 = (f32[512,512]{1,0:T(8,128)}, f32[512,512]{1,0:T(8,128)}, u32[]{:S(2)}, u32[]{:S(2)}) collective-permute-start(f32[512,512]{1,0:T(8,128)} %collective-permute-done.13.refs_7_), channel_id=1, source_target_pairs={{2,1},{6,5},{10,9},{14,13},{18,17},{22,21},{26,25},{30,29}} | collective-permute-start | bytes 3145736 | tf_op jit(solution)/shard_map/ppermute | solution.py:307
  33.0 2.3 %collective-permute-start.15 = (f32[512,512]{1,0:T(8,128)}, f32[512,512]{1,0:T(8,128)}, u32[]{:S(2)}, u32[]{:S(2)}) collective-permute-start(f32[512,512]{1,0:T(8,128)} %collective-permute-done.13.refs_7_), channel_id=1, source_target_pairs={{2,3},{6,7},{10,11},{14,15},{18,19},{22,23},{26,27},{30,31}} | collective-permute-start | bytes 3145736 | tf_op jit(solution)/shard_map/ppermute | solution.py:309
  35.3 6.4 %pick.8 = f32[576,512]{1,0:T(8,128)} custom-call(s32[256]{0:T(256)} %and_select_fusion.7.refs_0_, s32[160]{0:T(256)} %and_select_fusion.6.refs_1_, f32[512,1024]{1,0:T(8,128)S(1)} %copy-done, f32[512,1024]{1,0:T(8,128)} %collective-permute-done.6.refs_3_), custom_call_target="tpu_custom_call" | custom-call | tf_op jit(solution)/shard_map/pick/pallas_call | solution.py:69
  42.1 0.6 and_select_fusion.4.refs_1_.refs_0_
  42.6 6.3 %pick.9 = f32[256,1536]{1,0:T(8,128)} custom-call(s32[256]{0:T(256)} %and_select_fusion.7.refs_0_, s32[256]{0:T(256)} %and_select_fusion.4.refs_1_.refs_0_, f32[512,1024]{1,0:T(8,128)S(1)} %copy-done, f32[512,1024]{1,0:T(8,128)} %collective-permute-done.6.refs_3_), custom_call_target="tpu_custom_call" | custom-call | tf_op jit(solution)/shard_map/pick/pallas_call | solution.py:69
  49.0 1.3 collective-permute-start.10
  50.3 7.2 %collective-permute-done.7 = f32[576,512]{1,0:T(8,128)} collective-permute-done((f32[576,512]{1,0:T(8,128)}, f32[576,512]{1,0:T(8,128)}, u32[]{:S(2)}, u32[]{:S(2)}) %collective-permute-start.7) | collective-permute-done | bytes 1179680 | tf_op jit(solution)/shard_map/ppermute | solution.py:298
  57.5 2.9 %add.296 = f32[576,512]{1,0:T(8,128)} add(f32[576,512]{1,0:T(8,128)} %pick.8, f32[576,512]{1,0:T(8,128)} %collective-permute-done.7) | non-fusion elementwise | flops 294912 | bytes 3538944 | tf_op jit(solution)/shard_map/add | solution.py:298
  60.7 3.5 %add_select_fusion.4.refs_1_ = f32[512,512]{1,0:T(8,128)} fusion(f32[512,512]{1,0:T(8,128)S(1)} %fusion.39.one_ref.refs_6_, f32[512,512]{1,0:T(8,128)} %collective-permute-done.15.refs_9_, f32[512,512]{1,0:T(8,128)} %collective-permute-done.13.refs_7_, f32[512,512]{1,0:T(8,128)} %collective-permute-done.14.refs_8_, pred[]{:T(512)} %eq.271), kind=kLoop, calls=%fused_computation.79 | loop fusion | flops 786432 | bytes 5242881 | tf_op jit(solution)/shard_map/jit(_where)/select_n | solution.py:326
  64.2 1.9 collective-permute-start.16
  66.1 16.8 %collective-permute-done.10 = f32[256,1536]{1,0:T(8,128)} collective-permute-done((f32[256,1536]{1,0:T(8,128)}, f32[256,1536]{1,0:T(8,128)}, u32[]{:S(2)}, u32[]{:S(2)}) %collective-permute-start.10) | collective-permute-done | bytes 1572896 | tf_op jit(solution)/shard_map/ppermute | solution.py:298
  82.9 2.8 %add.299 = f32[256,1536]{1,0:T(8,128)} add(f32[256,1536]{1,0:T(8,128)S(1)} %copy-done.7, f32[256,1536]{1,0:T(8,128)} %collective-permute-done.10) | non-fusion elementwise | flops 393216 | bytes 4718592 | tf_op jit(solution)/shard_map/add | solution.py:298
  85.9 0.7 fusion.61
  86.7 1.4 collective-permute-done.8
  88.1 1.9 add.297.mine_ref
  90.0 4.4 %collective-permute-start.9 = (f32[576,512]{1,0:T(8,128)S(1)}, f32[576,512]{1,0:T(8,128)}, u32[]{:S(2)}, u32[]{:S(2)}) collective-permute-start(f32[576,512]{1,0:T(8,128)S(1)} %add.297.mine_ref), channel_id=1, source_target_pairs={{0,4},{4,0},{8,12},{12,8},{16,20},{20,16},{24,28},{28,24},{1,5},{5... | collective-permute-start | bytes 3538952 | tf_op jit(solution)/shard_map/ppermute | solution.py:290
  94.8 4.4 %pick.10 = f32[256,512]{1,0:T(8,128)} custom-call(s32[256]{0:T(256)} %and_select_fusion.4.refs_1_.refs_0_, f32[512,512]{1,0:T(8,128)} %add_select_fusion.4.refs_1_, f32[512,512]{1,0:T(8,128)} %collective-permute-done.16.refs_2_), custom_call_target="tpu_custom_call" | custom-call | tf_op jit(solution)/shard_map/pick/pallas_call | solution.py:69
  99.2 1.3 collective-permute-start.17
  100.7 1.0 slice_bitcast_fusion.1.lower_ref
  101.8 11.9 %collective-permute-done.17 = f32[256,512]{1,0:T(8,128)S(1)} collective-permute-done((f32[256,512]{1,0:T(8,128)}, f32[256,512]{1,0:T(8,128)S(1)}, u32[]{:S(2)}, u32[]{:S(2)}) %collective-permute-start.17) | collective-permute-done | bytes 524320 | tf_op jit(solution)/shard_map/ppermute | solution.py:298
  113.6 0.9 add.303
  114.8 3.2 %add.300.mine_ref = f32[256,1536]{1,0:T(8,128)} add(f32[256,1536]{1,0:T(8,128)} %add.299, f32[256,1536]{1,0:T(8,128)} %collective-permute-done.11) | non-fusion elementwise | flops 393216 | bytes 4718592 | tf_op jit(solution)/shard_map/add | solution.py:298
  118.0 2.8 %collective-permute-start.12 = (f32[256,1536]{1,0:T(8,128)}, f32[256,1536]{1,0:T(8,128)}, u32[]{:S(2)}, u32[]{:S(2)}) collective-permute-start(f32[256,1536]{1,0:T(8,128)} %add.300.mine_ref), channel_id=1, source_target_pairs={{0,4},{4,0},{8,12},{12,8},{16,20},{20,16},{24,28},{28,24},{1,5},{5... | collective-permute-start | bytes 4718600 | tf_op jit(solution)/shard_map/ppermute | solution.py:290
  120.8 0.8 select_reduce_fusion.6
  122.2 3.0 %slice_bitcast_fusion = (f32[512,512]{1,0:T(8,128)}, f32[512,512]{1,0:T(8,128)}) fusion(f32[2,512,512]{2,1,0:T(8,128)} %param.9), kind=kLoop, calls=%fused_computation.80 | loop fusion | bytes 4194304 | tf_op jit(solution)/shard_map/squeeze | solution.py:397
  125.2 8.1 %middle.1 = (f32[512,1024]{1,0:T(8,128)}, f32[296,512]{1,0:T(8,128)}, f32[296,512]{1,0:T(8,128)}, f32[512,512]{1,0:T(8,128)S(1)}) custom-call(s32[1]{0:T(128)} %bitcast.19.core_ref, s32[80]{0:T(128)} %get-tuple-element.353.slot_ref, s32[80]{0:T(128)} %get-tuple-element.354.target_ref.refs_1_, s32[1]{0:T(128)} %bitcast.18.count_ref.refs_2_, ...), custom_call_target="tpu_custom_call" | custom-call | tf_op jit(solution)/shard_map/middle/pallas_call | solution.py:125
  133.3 1.3 collective-permute-start.20
  134.6 1.3 collective-permute-start.23
  135.9 1.3 add.304.tm_ref
  137.2 0.8 copy-done.11
  138.0 13.8 %collective-permute-done.20.refs_11_ = f32[296,512]{1,0:T(8,128)} collective-permute-done((f32[296,512]{1,0:T(8,128)}, f32[296,512]{1,0:T(8,128)}, u32[]{:S(2)}, u32[]{:S(2)}) %collective-permute-start.20) | collective-permute-done | bytes 606240 | tf_op jit(solution)/shard_map/ppermute | solution.py:306
  151.8 2.1 %collective-permute-start.21 = (f32[296,512]{1,0:T(8,128)}, f32[296,512]{1,0:T(8,128)}, u32[]{:S(2)}, u32[]{:S(2)}) collective-permute-start(f32[296,512]{1,0:T(8,128)} %collective-permute-done.20.refs_11_), channel_id=1, source_target_pairs={{2,1},{6,5},{10,9},{14,13},{18,17},{22,21},{26,25},{30,29}} | collective-permute-start | bytes 1818632 | tf_op jit(solution)/shard_map/ppermute | solution.py:307
  153.9 2.1 %collective-permute-start.22 = (f32[296,512]{1,0:T(8,128)}, f32[296,512]{1,0:T(8,128)}, u32[]{:S(2)}, u32[]{:S(2)}) collective-permute-start(f32[296,512]{1,0:T(8,128)} %collective-permute-done.20.refs_11_), channel_id=1, source_target_pairs={{2,3},{6,7},{10,11},{14,15},{18,19},{22,23},{26,27},{30,31}} | collective-permute-start | bytes 1818632 | tf_op jit(solution)/shard_map/ppermute | solution.py:309
  156.1 8.7 %collective-permute-done.23.refs_15_ = f32[296,512]{1,0:T(8,128)} collective-permute-done((f32[296,512]{1,0:T(8,128)}, f32[296,512]{1,0:T(8,128)}, u32[]{:S(2)}, u32[]{:S(2)}) %collective-permute-start.23) | collective-permute-done | bytes 606240 | tf_op jit(solution)/shard_map/ppermute | solution.py:306
  164.8 2.1 %collective-permute-start.24 = (f32[296,512]{1,0:T(8,128)}, f32[296,512]{1,0:T(8,128)}, u32[]{:S(2)}, u32[]{:S(2)}) collective-permute-start(f32[296,512]{1,0:T(8,128)} %collective-permute-done.23.refs_15_), channel_id=1, source_target_pairs={{2,1},{6,5},{10,9},{14,13},{18,17},{22,21},{26,25},{30,29}} | collective-permute-start | bytes 1818632 | tf_op jit(solution)/shard_map/ppermute | solution.py:307
  166.9 0.8 copy-done.12
  167.8 2.1 %collective-permute-start.25 = (f32[296,512]{1,0:T(8,128)}, f32[296,512]{1,0:T(8,128)}, u32[]{:S(2)}, u32[]{:S(2)}) collective-permute-start(f32[296,512]{1,0:T(8,128)} %collective-permute-done.23.refs_15_), channel_id=1, source_target_pairs={{2,3},{6,7},{10,11},{14,15},{18,19},{22,23},{26,27},{30,31}} | collective-permute-start | bytes 1818632 | tf_op jit(solution)/shard_map/ppermute | solution.py:309
  169.9 0.7 convert_reduce_fusion.4
  171.3 0.6 reduce_max.9
  173.2 0.7 pad_add_fusion.6.where_ref.refs_0_
  173.8 9.2 %rows.1 = (bf16[1024,1024]{1,0:T(8,128)(2,1)S(1)}, bf16[1024,1024]{1,0:T(8,128)(2,1)S(1)}, f32[512,1024]{1,0:T(8,128)}) custom-call(s32[2]{0:T(128)} %pad_add_fusion.6.where_ref.refs_0_, f32[512,512]{1,0:T(8,128)S(1)} %get-tuple-element.633.panel_ref, f32[256,1536]{1,0:T(8,128)} %add.300.mine_ref, f32[256,1536]{1,0:T(8,128)} %collective-permute-done.12.mate_ref, ...), custom_call_target="tpu_custom_call" | custom-call | tf_op jit(solution)/shard_map/rows/pallas_call | solution.py:186
  183.1 10.3 %finish.1 = f32[512,1024]{1,0:T(8,128)} custom-call(s32[2]{0:T(128)} %pad_add_fusion.6.where_ref.refs_0_, s32[80]{0:T(128)} %get-tuple-element.354.target_ref.refs_1_, s32[1]{0:T(128)} %bitcast.18.count_ref.refs_2_, f32[512,1024]{1,0:T(8,128)} %get-tuple-element.343.refs_3_, bf16[1024,1024]{1,0:T(8,128)(2,1)S(1)} %get-tuple-element.634.refs_4_, ...), custom_call_target="tpu_custom_call" | custom-call | tf_op jit(solution)/shard_map/finish/pallas_call | solution.py:254
  (85 shorter events, 6.7 us)
Async XLA Ops:
  0.0 35.3 %copy-start = (f32[512,1024]{1,0:T(8,128)S(1)}, f32[512,1024]{1,0:T(8,128)}, u32[]{:S(2)}) copy-start(f32[512,1024]{1,0:T(8,128)} %refs_2_.3) | copy-start | bytes 6291460
  0.0 4.6 %copy-start.13 = (s32[2,512]{1,0:T(2,128)S(1)}, s32[2,512]{1,0:T(2,128)}, u32[]{:S(2)}) copy-start(s32[2,512]{1,0:T(2,128)} %param.7) | copy-start | bytes 12292
  0.0 35.3 %collective-permute-start.6 = (f32[512,1024]{1,0:T(8,128)}, f32[512,1024]{1,0:T(8,128)}, u32[]{:S(2)}, u32[]{:S(2)}) collective-permute-start(f32[512,1024]{1,0:T(8,128)} %refs_2_.3), channel_id=1, source_target_pairs={{0,4},{4,0},{8,12},{12,8},{16,20},{20,16},{24,28},{28,24},{1,5},{5... | collective-permute-start | bytes 6291464 | tf_op jit(solution)/shard_map/ppermute | solution.py:290
  3.2 57.4 %copy-start.6 = (f32[512,512]{1,0:T(8,128)}, f32[512,512]{1,0:T(8,128)S(1)}, u32[]{:S(2)}) copy-start(f32[512,512]{1,0:T(8,128)S(1)} %fusion.39.one_ref.refs_6_) | copy-start | bytes 3145732
  3.2 27.5 %collective-permute-start.13 = (f32[512,512]{1,0:T(8,128)S(1)}, f32[512,512]{1,0:T(8,128)}, u32[]{:S(2)}, u32[]{:S(2)}) collective-permute-start(f32[512,512]{1,0:T(8,128)S(1)} %fusion.39.one_ref.refs_6_), channel_id=1, source_target_pairs={{0,2},{4,6},{8,10},{12,14},{16,18},{20,22},{24,26},{28,30}} | collective-permute-start | bytes 3145736 | tf_op jit(solution)/shard_map/ppermute | solution.py:306
  30.7 29.9 %collective-permute-start.14 = (f32[512,512]{1,0:T(8,128)}, f32[512,512]{1,0:T(8,128)}, u32[]{:S(2)}, u32[]{:S(2)}) collective-permute-start(f32[512,512]{1,0:T(8,128)} %collective-permute-done.13.refs_7_), channel_id=1, source_target_pairs={{2,1},{6,5},{10,9},{14,13},{18,17},{22,21},{26,25},{30,29}} | collective-permute-start | bytes 3145736 | tf_op jit(solution)/shard_map/ppermute | solution.py:307
  33.0 27.6 %collective-permute-start.15 = (f32[512,512]{1,0:T(8,128)}, f32[512,512]{1,0:T(8,128)}, u32[]{:S(2)}, u32[]{:S(2)}) collective-permute-start(f32[512,512]{1,0:T(8,128)} %collective-permute-done.13.refs_7_), channel_id=1, source_target_pairs={{2,3},{6,7},{10,11},{14,15},{18,19},{22,23},{26,27},{30,31}} | collective-permute-start | bytes 3145736 | tf_op jit(solution)/shard_map/ppermute | solution.py:309
  41.8 15.7 %collective-permute-start.7 = (f32[576,512]{1,0:T(8,128)}, f32[576,512]{1,0:T(8,128)}, u32[]{:S(2)}, u32[]{:S(2)}) collective-permute-start(f32[576,512]{1,0:T(8,128)} %pick.8), channel_id=1, source_target_pairs={{0,8},{4,20},{8,0},{12,28},{16,24},{20,4},{24,16},{28,12},{1,9},{5... | collective-permute-start | bytes 3538952 | tf_op jit(solution)/shard_map/ppermute | solution.py:298
  49.0 33.9 %collective-permute-start.10 = (f32[256,1536]{1,0:T(8,128)}, f32[256,1536]{1,0:T(8,128)}, u32[]{:S(2)}, u32[]{:S(2)}) collective-permute-start(f32[256,1536]{1,0:T(8,128)} %pick.9), channel_id=1, source_target_pairs={{0,8},{4,20},{8,0},{12,28},{16,24},{20,4},{24,16},{28,12},{1,9},{5... | collective-permute-start | bytes 4718600 | tf_op jit(solution)/shard_map/ppermute | solution.py:298
  60.4 22.5 %copy-start.7 = (f32[256,1536]{1,0:T(8,128)S(1)}, f32[256,1536]{1,0:T(8,128)}, u32[]{:S(2)}) copy-start(f32[256,1536]{1,0:T(8,128)} %pick.9) | copy-start | bytes 4718596
  60.4 27.7 %collective-permute-start.8 = (f32[576,512]{1,0:T(8,128)}, f32[576,512]{1,0:T(8,128)}, u32[]{:S(2)}, u32[]{:S(2)}) collective-permute-start(f32[576,512]{1,0:T(8,128)} %add.296), channel_id=1, source_target_pairs={{0,16},{4,12},{8,24},{12,4},{16,0},{20,28},{24,8},{28,20},{1,17},{... | collective-permute-start | bytes 3538952 | tf_op jit(solution)/shard_map/ppermute | solution.py:298
  64.2 30.6 %collective-permute-start.16 = (f32[512,512]{1,0:T(8,128)}, f32[512,512]{1,0:T(8,128)}, u32[]{:S(2)}, u32[]{:S(2)}) collective-permute-start(f32[512,512]{1,0:T(8,128)} %add_select_fusion.4.refs_1_), channel_id=1, source_target_pairs={{0,4},{4,0},{8,12},{12,8},{16,20},{20,16},{24,28},{28,24},{1,5},{5... | collective-permute-start | bytes 3145736 | tf_op jit(solution)/shard_map/ppermute | solution.py:290
  85.7 29.1 %collective-permute-start.11 = (f32[256,1536]{1,0:T(8,128)}, f32[256,1536]{1,0:T(8,128)}, u32[]{:S(2)}, u32[]{:S(2)}) collective-permute-start(f32[256,1536]{1,0:T(8,128)} %add.299), channel_id=1, source_target_pairs={{0,16},{4,12},{8,24},{12,4},{16,0},{20,28},{24,8},{28,20},{1,17},{... | collective-permute-start | bytes 4718600 | tf_op jit(solution)/shard_map/ppermute | solution.py:298
  90.0 11.8 %copy-start.8 = (f32[576,512]{1,0:T(8,128)}, f32[576,512]{1,0:T(8,128)S(1)}, u32[]{:S(2)}) copy-start(f32[576,512]{1,0:T(8,128)S(1)} %add.297.mine_ref) | copy-start | bytes 3538948
  90.0 35.2 %collective-permute-start.9 = (f32[576,512]{1,0:T(8,128)S(1)}, f32[576,512]{1,0:T(8,128)}, u32[]{:S(2)}, u32[]{:S(2)}) collective-permute-start(f32[576,512]{1,0:T(8,128)S(1)} %add.297.mine_ref), channel_id=1, source_target_pairs={{0,4},{4,0},{8,12},{12,8},{16,20},{20,16},{24,28},{28,24},{1,5},{5... | collective-permute-start | bytes 3538952 | tf_op jit(solution)/shard_map/ppermute | solution.py:290
  94.8 5.9 %copy-start.9 = (f32[2,512,512]{2,1,0:T(8,128)S(1)}, f32[2,512,512]{2,1,0:T(8,128)}, u32[]{:S(2)}) copy-start(f32[2,512,512]{2,1,0:T(8,128)} %lower_ref.1) | copy-start | bytes 6291460
  99.2 14.4 %copy-start.10 = (f32[256,512]{1,0:T(8,128)S(1)}, f32[256,512]{1,0:T(8,128)}, u32[]{:S(2)}) copy-start(f32[256,512]{1,0:T(8,128)} %pick.10) | copy-start | bytes 1572868
  99.2 14.4 %collective-permute-start.17 = (f32[256,512]{1,0:T(8,128)}, f32[256,512]{1,0:T(8,128)S(1)}, u32[]{:S(2)}, u32[]{:S(2)}) collective-permute-start(f32[256,512]{1,0:T(8,128)} %pick.10), channel_id=1, source_target_pairs={{0,8},{4,20},{8,0},{12,28},{16,24},{20,4},{24,16},{28,12},{1,9},{5... | collective-permute-start | bytes 1572872 | tf_op jit(solution)/shard_map/ppermute | solution.py:298
  114.5 21.4 %collective-permute-start.18 = (f32[256,512]{1,0:T(8,128)}, f32[256,512]{1,0:T(8,128)}, u32[]{:S(2)}, u32[]{:S(2)}) collective-permute-start(f32[256,512]{1,0:T(8,128)} %add.303), channel_id=1, source_target_pairs={{0,16},{4,12},{8,24},{12,4},{16,0},{20,28},{24,8},{28,20},{1,17},{... | collective-permute-start | bytes 1572872 | tf_op jit(solution)/shard_map/ppermute | solution.py:298
  118.0 55.8 %collective-permute-start.12 = (f32[256,1536]{1,0:T(8,128)}, f32[256,1536]{1,0:T(8,128)}, u32[]{:S(2)}, u32[]{:S(2)}) collective-permute-start(f32[256,1536]{1,0:T(8,128)} %add.300.mine_ref), channel_id=1, source_target_pairs={{0,4},{4,0},{8,12},{12,8},{16,20},{20,16},{24,28},{28,24},{1,5},{5... | collective-permute-start | bytes 4718600 | tf_op jit(solution)/shard_map/ppermute | solution.py:290
  133.3 18.5 %collective-permute-start.20 = (f32[296,512]{1,0:T(8,128)}, f32[296,512]{1,0:T(8,128)}, u32[]{:S(2)}, u32[]{:S(2)}) collective-permute-start(f32[296,512]{1,0:T(8,128)} %get-tuple-element.347.refs_10_), channel_id=1, source_target_pairs={{0,2},{4,6},{8,10},{12,14},{16,18},{20,22},{24,26},{28,30}} | collective-permute-start | bytes 1818632 | tf_op jit(solution)/shard_map/ppermute | solution.py:306
  134.6 30.2 %collective-permute-start.23 = (f32[296,512]{1,0:T(8,128)}, f32[296,512]{1,0:T(8,128)}, u32[]{:S(2)}, u32[]{:S(2)}) collective-permute-start(f32[296,512]{1,0:T(8,128)} %get-tuple-element.348.refs_14_), channel_id=1, source_target_pairs={{0,2},{4,6},{8,10},{12,14},{16,18},{20,22},{24,26},{28,30}} | collective-permute-start | bytes 1818632 | tf_op jit(solution)/shard_map/ppermute | solution.py:306
  137.2 0.9 copy-start.11
  138.0 28.9 %collective-permute-start.19 = (f32[256,512]{1,0:T(8,128)S(1)}, f32[256,512]{1,0:T(8,128)S(1)}, u32[]{:S(2)}, u32[]{:S(2)}) collective-permute-start(f32[256,512]{1,0:T(8,128)S(1)} %add.304.tm_ref), channel_id=1, source_target_pairs={{0,4},{4,0},{8,12},{12,8},{16,20},{20,16},{24,28},{28,24},{1,5},{5... | collective-permute-start | bytes 1572872 | tf_op jit(solution)/shard_map/ppermute | solution.py:290
  151.8 31.3 %collective-permute-start.21 = (f32[296,512]{1,0:T(8,128)}, f32[296,512]{1,0:T(8,128)}, u32[]{:S(2)}, u32[]{:S(2)}) collective-permute-start(f32[296,512]{1,0:T(8,128)} %collective-permute-done.20.refs_11_), channel_id=1, source_target_pairs={{2,1},{6,5},{10,9},{14,13},{18,17},{22,21},{26,25},{30,29}} | collective-permute-start | bytes 1818632 | tf_op jit(solution)/shard_map/ppermute | solution.py:307
  153.9 29.1 %collective-permute-start.22 = (f32[296,512]{1,0:T(8,128)}, f32[296,512]{1,0:T(8,128)}, u32[]{:S(2)}, u32[]{:S(2)}) collective-permute-start(f32[296,512]{1,0:T(8,128)} %collective-permute-done.20.refs_11_), channel_id=1, source_target_pairs={{2,3},{6,7},{10,11},{14,15},{18,19},{22,23},{26,27},{30,31}} | collective-permute-start | bytes 1818632 | tf_op jit(solution)/shard_map/ppermute | solution.py:309
  164.8 18.3 %collective-permute-start.24 = (f32[296,512]{1,0:T(8,128)}, f32[296,512]{1,0:T(8,128)}, u32[]{:S(2)}, u32[]{:S(2)}) collective-permute-start(f32[296,512]{1,0:T(8,128)} %collective-permute-done.23.refs_15_), channel_id=1, source_target_pairs={{2,1},{6,5},{10,9},{14,13},{18,17},{22,21},{26,25},{30,29}} | collective-permute-start | bytes 1818632 | tf_op jit(solution)/shard_map/ppermute | solution.py:307
  166.9 0.8 copy-start.12
  167.8 15.3 %collective-permute-start.25 = (f32[296,512]{1,0:T(8,128)}, f32[296,512]{1,0:T(8,128)}, u32[]{:S(2)}, u32[]{:S(2)}) collective-permute-start(f32[296,512]{1,0:T(8,128)} %collective-permute-done.23.refs_15_), channel_id=1, source_target_pairs={{2,3},{6,7},{10,11},{14,15},{18,19},{22,23},{26,27},{30,31}} | collective-permute-start | bytes 1818632 | tf_op jit(solution)/shard_map/ppermute | solution.py:309
  183.0 10.3 %copy-start.2 = (bf16[1024,1024]{1,0:T(8,128)(2,1)}, bf16[1024,1024]{1,0:T(8,128)(2,1)S(1)}, u32[]{:S(2)}) copy-start(bf16[1024,1024]{1,0:T(8,128)(2,1)S(1)} %get-tuple-element.634.refs_4_) | copy-start | bytes 6291460
  183.1 10.3 %copy-start.3 = (bf16[1024,1024]{1,0:T(8,128)(2,1)}, bf16[1024,1024]{1,0:T(8,128)(2,1)S(1)}, u32[]{:S(2)}) copy-start(bf16[1024,1024]{1,0:T(8,128)(2,1)S(1)} %get-tuple-element.635.refs_5_) | copy-start | bytes 6291460
where the time goes:
time: 194 us
  waiting for transfers between devices  80 us (41%)
  Pallas kernels  44.7 us (23%)
  starting transfers between devices  30.4 us (16%)
  other arithmetic  26.4 us (14%)
  local copies, waits for them, and re-layouts  6.55 us (3%)
  between operations  3 us (2%)
  matrix products  2.54 us (1%)
    ppermute x3, waiting for transfers between devices, relay(): lax.ppermute(x if even == 2 else parts[-2 if even > 4 else 1], 'pcol', [(...  42.6 us
    ppermute x6, waiting for transfers between devices, gather_sum(): lax.ppermute(x, 'prow', [(i, i ^ (second if i % 2 else first)) for i in r...  37.3 us
    pallas_call x3, Pallas kernels, pick(): pl.pallas_call(body, out_shape=jax.ShapeDtypeStruct(shape, F32), in_specs...  17.2 us
    add x6, other arithmetic, gather_sum(): x + lax.ppermute(x, 'prow', [(i, i ^ (second if i % 2 else first)) for i...  12.9 us
    pallas_call x1, Pallas kernels, finish_step(): pl.pallas_call(body, out_shape=jax.ShapeDtypeStruct((rows, cols), F32), i...  10.3 us
    ppermute x5, starting transfers between devices, swap_cores(): lax.ppermute(x, 'prow', [(i, i ^ 1) for i in range(lax.axis_size('prow'))])  9.78 us
    pallas_call x1, Pallas kernels, row_step(): pl.pallas_call(body, out_shape=(jax.ShapeDtypeStruct((2 * width, cols), B...  9.21 us
    pallas_call x1, Pallas kernels, middle_step(): pl.pallas_call(body, out_shape=(shape(rows, cols), shape(part, width), sh...  8.06 us
  transfers between devices with their start and end apart: 20, of which 7 were waited for; matrix products, arithmetic and copies ran while one was open for 17% of the time, Pallas kernels for 18%

commit v1 on v0

--- a/solution.py
+++ b/solution.py
@@ -9,7 +9,12 @@
 SHARE = 80
 F32, BF16 = jnp.float32, jnp.bfloat16
 SMEM, VMEM, ANY = (pl.BlockSpec(memory_space=space) for space in (pltpu.SMEM, pltpu.VMEM, pl.ANY))
+COSTS = dict(middle=6000000000, rows=10000000000, finish=10000000000, place=1)
 PARAMS = pltpu.CompilerParams(vmem_limit_bytes=56 << 20)
+
+
+def cost(work):
+    return pl.CostEstimate(flops=work, bytes_accessed=1, transcendentals=0)
 
 
 def split(x):
@@ -42,49 +47,72 @@
     return (source, outside)
 
 
-def pick(own, mate, lists, pieces, shape):
-    rows, cols = own.shape
-    count = len(lists)
+def pick(sources, lists, pieces, shapes, choice=None, work=1):
+    rows, cols = sources[0].shape
+    count, many = len(lists), len(sources)
+    stacked = 1 if choice else many
 
     def body(*refs):
-        index_refs, (own_ref, mate_ref, out_ref, chip, sems) = refs[:count], refs[count:]
-        copies = [
-            pltpu.make_async_copy(own_ref, chip.at[pl.ds(0, rows)], sems.at[0]),
-            pltpu.make_async_copy(mate_ref, chip.at[pl.ds(rows, rows)], sems.at[1]),
-        ]
-        for copy in copies:
-            copy.start()
-        for copy in copies:
-            copy.wait()
-        for number, source, row, column, width in pieces:
+        index_refs, source_refs, rest = refs[:count], refs[count : count + many], refs[count + many :]
+        if choice:
+            where_ref, rest = rest[0], rest[1:]
+        out_refs, (chip, sems) = rest[: len(shapes)], rest[len(shapes) :]
+        if choice:
+            for ref, places in zip(source_refs, choice[1]):
+
+                @pl.when(among(where_ref[1], places))
+                def _():
+                    copy = pltpu.make_async_copy(ref, chip, sems.at[0])
+                    copy.start()
+                    copy.wait()
+        else:
+            copies = [
+                pltpu.make_async_copy(ref, chip.at[pl.ds(k * rows, rows)], sems.at[k])
+                for k, ref in enumerate(source_refs)
+            ]
+            for copy in copies:
+                copy.start()
+            for copy in copies:
+                copy.wait()
+        for index_ref, vector, segments in zip(index_refs, lists, pieces):
 
             def step(i, carry):
-                wanted = index_refs[number][i]
-                value = chip[pl.ds(jnp.maximum(wanted, 0), 1), source : source + width]
-                out_ref[pl.ds(row + i, 1), column : column + width] = jnp.where(wanted >= 0, value, 0.0)
+                wanted = index_ref[i]
+                at = pl.ds(jnp.maximum(wanted, 0), 1)
+                for output, source, row, column, width in segments:
+                    value = jnp.where(wanted >= 0, chip[at, source : source + width], 0.0)
+                    out_refs[output][pl.ds(row + i, 1), column : column + width] = value
                 return carry
 
-            lax.fori_loop(0, lists[number].shape[0], step, 0, unroll=8)
+            lax.fori_loop(0, vector.shape[0], step, 0, unroll=8)
 
     return pl.pallas_call(
         body,
-        out_shape=jax.ShapeDtypeStruct(shape, F32),
-        in_specs=[SMEM] * count + [ANY, ANY],
-        out_specs=VMEM,
-        scratch_shapes=[pltpu.VMEM((2 * rows, cols), F32), pltpu.SemaphoreType.DMA((2,))],
+        out_shape=[jax.ShapeDtypeStruct(shape, F32) for shape in shapes],
+        in_specs=[SMEM] * count + [ANY] * many + ([SMEM] if choice else []),
+        out_specs=[VMEM] * len(shapes),
+        scratch_shapes=[pltpu.VMEM((stacked * rows, cols), F32), pltpu.SemaphoreType.DMA((stacked,))],
         compiler_params=PARAMS,
+        cost_estimate=cost(work),
         name="pick",
-    )(*lists, own, mate)
-
-
-def middle_step(matrix, one, mine, mate, lower, upper_one, upper_two, core, slots, targets, count, size):
+    )(*lists, *sources, *([choice[0]] if choice else []))
+
+
+def among(value, places):
+    found = value == places[0]
+    for place in places[1:]:
+        found = found | (value == place)
+    return found
+
+
+def middle_step(matrix, one, mine, mate, lower, upper, core, slots, targets, count, size):
     rows, cols = matrix.shape
-    width = lower.shape[0]
+    width = lower.shape[1]
     half = width // 2
     blocks = cols // width
     part = (rows + SHARE) // 2
 
-    def body(core_ref, slot_ref, target_ref, count_ref, matrix_ref, one_ref, mine_ref, mate_ref, lower_ref, u1_ref, u2_ref,
+    def body(core_ref, slot_ref, target_ref, count_ref, matrix_ref, one_ref, mine_ref, mate_ref, lower_ref, u_ref,
              block_ref, upper_ref, under_ref, panel_ref, raw, pair, new_one):
         block_ref[...] = matrix_ref[...]
         raw[...] = jnp.zeros_like(raw)
@@ -101,7 +129,7 @@
             return carry
 
         lax.fori_loop(0, count_ref[0], bring, 0)
-        fresh = mul(split(raw[...]), split(u1_ref[...]))
+        fresh = mul(split(raw[...]), split(u_ref[0]))
         pair[pl.ds(rows, SHARE), :] = fresh
         new_one[...] = one_ref[...]
 
@@ -112,12 +140,12 @@
         lax.fori_loop(0, count_ref[0], renew, 0)
         first = pl.multiple_of(core_ref[0] * half, half)
         second = pl.multiple_of(half - core_ref[0] * half, half)
-        panel = mul(split(lower_ref[:, pl.ds(first, half)]), split(mine_ref[:half, :])) + mul(
-            split(lower_ref[:, pl.ds(second, half)]), split(mate_ref[:half, :])
+        panel = mul(split(lower_ref[0, :, pl.ds(first, half)]), split(mine_ref[:half, :])) + mul(
+            split(lower_ref[0, :, pl.ds(second, half)]), split(mate_ref[:half, :])
         )
         panel_ref[...] = panel
         rest = block_ref[:, width : 2 * width] - mul(split(new_one[...]), split(panel))
-        pair[pl.ds(0, rows), :] = mul(split(rest), split(u2_ref[...]))
+        pair[pl.ds(0, rows), :] = mul(split(rest), split(u_ref[1]))
         upper_ref[...] = pair[:part, :]
         under_ref[...] = pair[part:, :]
 
@@ -125,12 +153,13 @@
     return pl.pallas_call(
         body,
         out_shape=(shape(rows, cols), shape(part, width), shape(part, width), shape(width, width)),
-        in_specs=[SMEM] * 4 + [VMEM] * 7,
+        in_specs=[SMEM] * 4 + [VMEM] * 6,
         out_specs=(VMEM,) * 4,
         scratch_shapes=[pltpu.VMEM(s, F32) for s in ((SHARE, width), (rows + SHARE, width), (rows, width))],
         compiler_params=PARAMS,
+        cost_estimate=cost(COSTS["middle"]),
         name="middle",
-    )(core, slots, targets, count, matrix, one, mine, mate, lower, upper_one, upper_two)
+    )(core, slots, targets, count, matrix, one, mine, mate, lower, upper)
 
 
 def row_step(where, panel, mine, mate, top_mine, top_mate, lower, cols):
@@ -194,6 +223,7 @@
         out_specs=(VMEM,) * 3,
         scratch_shapes=[pltpu.VMEM((width, width), F32)],
         compiler_params=PARAMS,
+        cost_estimate=cost(COSTS["rows"]),
         name="rows",
     )(where, panel, mine, mate, top_mine, top_mate, lower)
 
@@ -212,11 +242,8 @@
         me, column = where_ref[0], where_ref[1]
         first_column = column == 0
         for k in range(parts):
-            mine = column == held[k][0]
-            for z in held[k][1:]:
-                mine = mine | (column == z)
-
-            @pl.when((me >= 2) & mine)
+
+            @pl.when((me >= 2) & among(column, held[k]))
             def _():
                 copies = [
                     pltpu.make_async_copy(one_refs[k], one, sems.at[0]),
@@ -262,6 +289,7 @@
             pltpu.SemaphoreType.DMA((3,)),
         ],
         compiler_params=PARAMS,
+        cost_estimate=cost(COSTS["finish"]),
         name="finish",
     )(where, targets, count, block, high, low, *ones, *uppers, *unders, edge)
 
@@ -282,6 +310,7 @@
         in_specs=[SMEM, SMEM, VMEM, VMEM],
         out_specs=VMEM,
         compiler_params=PARAMS,
+        cost_estimate=cost(COSTS["place"]),
         name="place",
     )(where_to, count, target, rows)
 
@@ -290,24 +319,44 @@
     return lax.ppermute(x, "prow", [(i, i ^ 1) for i in range(lax.axis_size("prow"))])
 
 
-def gather_sum(x):
-    devices = lax.axis_size("prow")
-    bits = [1 << k for k in range(1, devices.bit_length() - 1)]
-    turned = bits[len(bits) // 2 :] + bits[: len(bits) // 2]
-    for first, second in zip(bits, turned):
-        x = x + lax.ppermute(x, "prow", [(i, i ^ (second if i % 2 else first)) for i in range(devices)])
+def axes_order():
+    bits = [1 << k for k in range(1, lax.axis_size("prow").bit_length() - 1)]
+    return list(zip(bits, bits[len(bits) // 2 :] + bits[: len(bits) // 2]))
+
+
+def flip_axes(x, pair):
+    first, second = pair
+    return lax.ppermute(x, "prow", [(i, i ^ (second if i % 2 else first)) for i in range(lax.axis_size("prow"))])
+
+
+def gather_sum(x, steps=None):
+    for pair in axes_order() if steps is None else steps:
+        x = x + flip_axes(x, pair)
     return x, swap_cores(x)
 
 
-def relay(x):
+def first_hop(x):
+    return lax.ppermute(x, "pcol", [(0, 2)])
+
+
+def onward(x, current):
     count = lax.axis_size("pcol")
     parts = [x]
     for even in range(2, count, 2):
-        current = lax.ppermute(x if even == 2 else parts[-2 if even > 4 else 1], "pcol", [(even - 2, even)])
         parts += [current, lax.ppermute(current, "pcol", [(even, even - 1)])]
-        if even + 2 >= count and even + 1 < count:
+        if even + 2 < count:
+            current = lax.ppermute(current, "pcol", [(even, even + 2)])
+        elif even + 1 < count:
             parts.append(lax.ppermute(current, "pcol", [(even, even + 1)]))
     return parts
+
+
+def relay(x):
+    return onward(x, first_hop(x))
+
+
+def after(x, *others):
+    return lax.optimization_barrier((x, *others))[0]
 
 
 def held_by(count):
@@ -340,7 +389,7 @@
     mate = swap_cores(matrix)
 
     column_one = product(matrix[:, :width], upper_inv[0])
-    ones = relay(column_one)
+    hop = first_hop(column_one)
 
     named, taken = pivots[0], pivots[1]
     source_one, outside_one = displaced(named, 0)
@@ -390,24 +439,51 @@
 
     origins, own_slot, own_row, count = batch(0, BATCH)
     size = BATCH // 2
-    lists = [ours(named), origins]
-    pieces = [(0, width, 0, 0, width)] + [(1, b * width, half + b * size, 0, width) for b in range(blocks)]
-    mine, mates = gather_sum(pick(matrix, mate, lists, pieces, (half + blocks * size, width)))
+    where = jnp.stack([me, column]).astype(jnp.int32)
+    held = held_by(lax.axis_size("pcol"))
+    near, far = ours(named), ours(second_rows)
+    segments = [
+        [(0, width, 0, 0, width)],
+        [(0, b * width, half + b * size, 0, width) for b in range(blocks)],
+    ]
+    (mine,) = pick([matrix, mate], [after(near, column_one), origins], segments, [(half + blocks * size, width)], work=1)
+    segments = [
+        [(0, 0, 0, 0, width)] + ([(0, 2 * width, 0, width, cols - 2 * width)] if blocks > 2 else []),
+        [(0, 0, 0, cols - width, cols)],
+    ]
+    (rest,) = pick([matrix, mate], [after(near, mine, hop), far], segments, [(half, 2 * cols - width)], work=6000000000)
+    ones = onward(column_one, hop)
+    first, *others = axes_order()
+    arriving = flip_axes(mine, first)
+    mine = mine + arriving
+    mine, mates = gather_sum(mine, others)
+
+    wanted = second_rows - me * rows
+    wanted = jnp.where((wanted >= 0) & (wanted < rows), wanted, -1)
+    keep, give = jnp.where(core == 0, wanted[:half], wanted[half:]), jnp.where(core == 0, wanted[half:], wanted[:half])
+    top, given = pick(
+        ones, [after(keep, mine), give], [[(0, 0, 0, 0, width)], [(1, 0, 0, 0, width)]], [(half, width)] * 2, (where, held), 6000000000
+    )
     block, upper, under, panel = middle_step(
-        matrix, column_one, mine, mates, lower_inv[0], upper_inv[0], upper_inv[1], core[None], own_slot, own_row, count, size
+        matrix, after(column_one, top), mine, mates, lower_inv, upper_inv, core[None], own_slot, own_row, count, size
     )
-    uppers, unders = relay(upper), relay(under)
-
-    lists = [ours(named), ours(second_rows)]
-    pieces = [(0, 0, 0, 0, width)] + [(0, b * width, 0, (b - 1) * width, width) for b in range(2, blocks)]
-    pieces += [(1, 0, 0, cols - width, cols)]
-    mine, mates = gather_sum(pick(matrix, mate, lists, pieces, (half, 2 * cols - width)))
-
-    one = joined(ones)
-    top_mine, top_mate = gather_sum(pick(one, swap_cores(one), [ours(second_rows)], [(0, 0, 0, 0, width)], (half, width)))
-    where = jnp.stack([me, column]).astype(jnp.int32)
-    high, low, edge = row_step(where, panel, mine, mates, top_mine, top_mate, lower_inv, cols)
-    held = held_by(lax.axis_size("pcol"))
+    hops = first_hop(upper), first_hop(under)
+    given = swap_cores(given)
+    top = after(top, upper) + given
+    rest = after(rest, mine)
+    arriving = flip_axes(rest, first)
+    rest = after(rest, upper) + arriving
+    uppers = onward(upper, after(hops[0], rest))
+    arriving = flip_axes(top, first)
+    top = after(top, hops[0]) + arriving
+    unders = onward(under, after(hops[1], top))
+    for pair in others:
+        arriving = flip_axes(rest, pair)
+        rest = after(rest, hops[1]) + arriving
+        top = top + flip_axes(top, pair)
+    rest_mine, rest_mates = rest, swap_cores(rest)
+    top_mine, top_mate = top, swap_cores(top)
+    high, low, edge = row_step(where, after(panel, *uppers[1:]), rest_mine, rest_mates, top_mine, top_mate, lower_inv, cols)
     result = finish_step(where, own_row, count, block, ones, uppers, unders, high, low, edge, held)
 
     crowded = (moved > BATCH) | (jnp.max(shares) > SHARE)
@@ -415,7 +491,7 @@
 
     def more(number, result):
         origins, own_slot, own_row, count = batch(number * SHARE, SHARE)
-        rows_here = gather_sum(pick(matrix, mate, [origins], [(0, 0, 0, 0, cols)], (SHARE // 2, cols)))
+        rows_here = gather_sum(pick([matrix, mate], [origins], [[(0, 0, 0, 0, cols)]], [(SHARE // 2, cols)])[0])
         raw = jnp.take(jnp.concatenate(rows_here, axis=0), own_slot, axis=0)
         one = product(raw[:, :width], upper_inv[0])
         two = product(raw[:, width : 2 * width] - product(one, panel), upper_inv[1])

time: 194 us -> 163 us (0.84); the launches traced: 194 us -> 160 us
  waiting for transfers between devices: 80 us -> 53.9 us
  other arithmetic: 26.4 us -> 18.4 us
  starting transfers between devices: 30.4 us -> 34 us
  local copies, waits for them, and re-layouts: 6.55 us -> 3.47 us
    ppermute x15, waiting for transfers between devices: 80 us -> 53.6 us  [the longest x6 26.7 us: flip_axes(): lax.ppermute(x, 'prow', [(i, i ^ (second if i % 2 else first)) for i in r...]
    add x6 -> x7, other arithmetic: 12.9 us -> 7.16 us  [the longest x1 1.75 us: shards(): rest = after(rest, upper) + arriving]
    squeeze x2 -> x0, local copies, waits for them, and re-layouts: 4.07 us -> none  [the longest x1 3.04 us: shards(): upper_inv[1]]
    ppermute x5, starting transfers between devices: 9.78 us -> 13.2 us  [swap_cores(): lax.ppermute(x, 'prow', [(i, i ^ 1) for i in range(lax.axis_size('prow'))])]
    select_n x1 -> x2, other arithmetic: 3.49 us -> 0.6 us  [the longest x1 0.6 us: shards(): jnp.where(core == 0, wanted[half:], wanted[:half])]
  transfers between devices with their start and end apart: 20 -> 20, of which waited for: 7 -> 10; matrix products, arithmetic and copies ran while one was open for 17% -> 14% of each run, Pallas kernels for 18% -> 18%
where the time goes in v1:
time: 163 us; the launch traced here: 160 us
  waiting for transfers between devices  53.9 us (33%)
  Pallas kernels  43.8 us (27%)
  starting transfers between devices  34 us (21%)
  other arithmetic  18.4 us (11%)
  matrix products  3.52 us (2%)
  local copies, waits for them, and re-layouts  3.47 us (2%)
  between operations  2.95 us (2%)
    ppermute x6, waiting for transfers between devices, flip_axes(): lax.ppermute(x, 'prow', [(i, i ^ (second if i % 2 else first)) for i in r...  26.7 us
    pallas_call x3, Pallas kernels, pick(): pl.pallas_call(body, out_shape=[jax.ShapeDtypeStruct(shape, F32) for shap...  17.8 us
    ppermute x3, waiting for transfers between devices, first_hop(): return lax.ppermute(x, 'pcol', [(0, 2)])  15.5 us
    ppermute x5, starting transfers between devices, swap_cores(): lax.ppermute(x, 'prow', [(i, i ^ 1) for i in range(lax.axis_size('prow'))])  13.2 us
    pallas_call x1, Pallas kernels, row_step(): pl.pallas_call(body, out_shape=(jax.ShapeDtypeStruct((2 * width, cols), B...  9.26 us
    pallas_call x1, Pallas kernels, finish_step(): pl.pallas_call(body, out_shape=jax.ShapeDtypeStruct((rows, cols), F32), i...  8.77 us
    pallas_call x1, Pallas kernels, middle_step(): pl.pallas_call(body, out_shape=(shape(rows, cols), shape(part, width), sh...  8.02 us
    ppermute x3, waiting for transfers between devices, onward(): parts += [current, lax.ppermute(current, 'pcol', [(even, even - 1)])]  6.96 us
  transfers between devices with their start and end apart: 20, of which 10 were waited for; matrix products, arithmetic and copies ran while one was open for 14% of the time, Pallas kernels for 18%

profile of v1, /device:TPU:23, one launch (start us, length us, event | category | flops | bytes accessed | tf_op | source)
XLA Modules:
  0.0 160.0 jit_solution(638165798155954545)
XLA Ops:
  0.0 0.7 collective-permute-start.6
  0.7 0.8 fusion.66
  1.9 0.8 compare_reduce_fusion.5
  3.1 3.5 %fusion.39.refs_2_.one_ref.refs_6_ = f32[512,512]{1,0:T(8,128)} fusion(f32[2,512,512]{2,1,0:T(8,128)} %u_ref.1, f32[512,1024]{1,0:T(8,128)} %refs_2_.3), kind=kOutput, calls=%fused_computation.79 | convolution fusion | flops 805306368 | bytes 3145728 | tf_op jit(solution)/shard_map/dot_general | solution.py:31
  11.1 0.7 and_select_fusion.6.refs_1_
  11.8 5.8 %pick.8 = f32[576,512]{1,0:T(8,128)} custom-call(s32[256]{0:T(256)} %and_select_fusion.7.refs_0_, s32[160]{0:T(256)} %and_select_fusion.6.refs_1_, f32[512,1024]{1,0:T(8,128)S(1)} %copy-done, f32[512,1024]{1,0:T(8,128)} %collective-permute-done.6.refs_3_), custom_call_target="tpu_custom_call" | custom-call | flops 1 | bytes 1 | tf_op jit(solution)/shard_map/pick/pallas_call | solution.py:89
  17.9 1.3 collective-permute-start.9
  19.2 14.2 %collective-permute-done.7 = f32[576,512]{1,0:T(8,128)S(1)} collective-permute-done((f32[576,512]{1,0:T(8,128)}, f32[576,512]{1,0:T(8,128)S(1)}, u32[]{:S(2)}, u32[]{:S(2)}) %collective-permute-start.7) | collective-permute-done | bytes 1179680 | tf_op jit(solution)/shard_map/ppermute | solution.py:329
  33.4 1.5 add.289
  35.2 0.7 fusion.63
  37.0 8.3 %collective-permute-done.9.refs_3_.refs_7_ = f32[512,512]{1,0:T(8,128)} collective-permute-done((f32[512,512]{1,0:T(8,128)}, f32[512,512]{1,0:T(8,128)}, u32[]{:S(2)}, u32[]{:S(2)}) %collective-permute-start.9) | collective-permute-done | bytes 1048608 | tf_op jit(solution)/shard_map/ppermute | solution.py:339
  45.3 2.3 %collective-permute-start.10 = (f32[512,512]{1,0:T(8,128)}, f32[512,512]{1,0:T(8,128)}, u32[]{:S(2)}, u32[]{:S(2)}) collective-permute-start(f32[512,512]{1,0:T(8,128)} %collective-permute-done.9.refs_3_.refs_7_), channel_id=1, source_target_pairs={{2,1},{6,5},{10,9},{14,13},{18,17},{22,21},{26,25},{30,29}} | collective-permute-start | bytes 3145736 | tf_op jit(solution)/shard_map/ppermute | solution.py:346
  47.7 2.3 %collective-permute-start.11 = (f32[512,512]{1,0:T(8,128)}, f32[512,512]{1,0:T(8,128)}, u32[]{:S(2)}, u32[]{:S(2)}) collective-permute-start(f32[512,512]{1,0:T(8,128)} %collective-permute-done.9.refs_3_.refs_7_), channel_id=1, source_target_pairs={{2,3},{6,7},{10,11},{14,15},{18,19},{22,23},{26,27},{30,31}} | collective-permute-start | bytes 3145736 | tf_op jit(solution)/shard_map/ppermute | solution.py:350
  50.6 1.5 add.290.mine_ref
  52.1 1.6 collective-permute-start.12
  53.7 6.3 %pick.10 = f32[256,1536]{1,0:T(8,128)} custom-call(s32[256]{0:T(256)} %and_select_fusion.7.refs_0_, s32[256]{0:T(256)} %and_select_fusion.4.refs_1_, f32[512,1024]{1,0:T(8,128)S(1)} %copy-done, f32[512,1024]{1,0:T(8,128)} %collective-permute-done.6.refs_3_), custom_call_target="tpu_custom_call" | custom-call | flops 6000000000 | bytes 1 | tf_op jit(solution)/shard_map/pick/pallas_call | solution.py:89
  60.1 0.8 collective-permute-start.14
  60.9 0.6 pad_add_fusion.6.refs_6_.where_ref.refs_0_
  61.4 0.8 select_reduce_fusion.6
  62.2 0.6 broadcast_select_fusion.3
  62.8 5.6 %collective-permute-done.10.refs_4_.refs_8_ = f32[512,512]{1,0:T(8,128)} collective-permute-done((f32[512,512]{1,0:T(8,128)}, f32[512,512]{1,0:T(8,128)}, u32[]{:S(2)}, u32[]{:S(2)}) %collective-permute-start.10) | collective-permute-done | bytes 1048608 | tf_op jit(solution)/shard_map/ppermute | solution.py:346
  68.4 2.3 %collective-permute-done.11.refs_5_.refs_9_ = f32[512,512]{1,0:T(8,128)} collective-permute-done((f32[512,512]{1,0:T(8,128)}, f32[512,512]{1,0:T(8,128)}, u32[]{:S(2)}, u32[]{:S(2)}) %collective-permute-start.11) | collective-permute-done | bytes 1048608 | tf_op jit(solution)/shard_map/ppermute | solution.py:350
  70.7 5.6 %pick.9 = (f32[256,512]{1,0:T(8,128)}, f32[256,512]{1,0:T(8,128)}) custom-call(s32[256]{0:T(256)} %get-tuple-element.358.refs_0_, s32[256]{0:T(256)} %get-tuple-element.466.refs_1_, f32[512,512]{1,0:T(8,128)} %fusion.39.refs_2_.one_ref.refs_6_, f32[512,512]{1,0:T(8,128)} %collective-permute-done.9.refs_3_.refs_7_, ...), custom_call_target="tpu_custom_call" | custom-call | flops 6000000000 | bytes 1 | tf_op jit(solution)/shard_map/pick/pallas_call | solution.py:89
  76.4 1.1 copy-done.11
  77.4 8.0 %middle.1 = (f32[512,1024]{1,0:T(8,128)}, f32[296,512]{1,0:T(8,128)}, f32[296,512]{1,0:T(8,128)}, f32[512,512]{1,0:T(8,128)S(1)}) custom-call(s32[1]{0:T(128)} %bitcast.19.core_ref, s32[80]{0:T(128)} %get-tuple-element.381.slot_ref, s32[80]{0:T(128)} %get-tuple-element.382.target_ref.refs_1_, s32[1]{0:T(128)} %bitcast.18.count_ref.refs_2_, ...), custom_call_target="tpu_custom_call" | custom-call | flops 6000000000 | bytes 1 | tf_op jit(solution)/shard_map/middle/pallas_call | solution.py:153
  85.5 1.8 %add.292 = f32[256,1536]{1,0:T(8,128)S(1)} add(f32[256,1536]{1,0:T(8,128)S(1)} %copy-done.7, f32[256,1536]{1,0:T(8,128)} %collective-permute-done.14) | non-fusion elementwise | flops 393216 | bytes 4718592 | tf_op jit(solution)/shard_map/add | solution.py:475
  87.3 1.3 collective-permute-start.17
  88.7 3.9 %collective-permute-start.20 = (f32[256,512]{1,0:T(8,128)S(1)}, f32[256,512]{1,0:T(8,128)S(1)}, u32[]{:S(2)}, u32[]{:S(2)}) collective-permute-start(f32[256,512]{1,0:T(8,128)S(1)} %copy-done.15), channel_id=1, source_target_pairs={{0,4},{4,0},{8,12},{12,8},{16,20},{20,16},{24,28},{28,24},{1,5},{5... | collective-permute-start | bytes 1572872 | tf_op jit(solution)/shard_map/ppermute | solution.py:319
  92.6 1.3 collective-permute-start.13
  94.3 7.2 %collective-permute-done.17.refs_15_ = f32[296,512]{1,0:T(8,128)S(1)} collective-permute-done((f32[296,512]{1,0:T(8,128)S(1)}, f32[296,512]{1,0:T(8,128)S(1)}, u32[]{:S(2)}, u32[]{:S(2)}) %collective-permute-start.17) | collective-permute-done | bytes 606240 | tf_op jit(solution)/shard_map/ppermute | solution.py:339
  101.5 0.8 copy-done.14
  102.3 10.3 %collective-permute-done.18 = f32[256,1536]{1,0:T(8,128)S(1)} collective-permute-done((f32[256,1536]{1,0:T(8,128)S(1)}, f32[256,1536]{1,0:T(8,128)S(1)}, u32[]{:S(2)}, u32[]{:S(2)}) %collective-permute-start.18) | collective-permute-done | bytes 1572896 | tf_op jit(solution)/shard_map/ppermute | solution.py:329
  112.6 1.3 add.293.mine_ref
  113.9 2.6 %collective-permute-start.19 = (f32[256,1536]{1,0:T(8,128)}, f32[256,1536]{1,0:T(8,128)}, u32[]{:S(2)}, u32[]{:S(2)}) collective-permute-start(f32[256,1536]{1,0:T(8,128)} %add.293.mine_ref), channel_id=1, source_target_pairs={{0,4},{4,0},{8,12},{12,8},{16,20},{20,16},{24,28},{28,24},{1,5},{5... | collective-permute-start | bytes 4718600 | tf_op jit(solution)/shard_map/ppermute | solution.py:319
  116.6 1.9 %collective-permute-start.22 = (f32[256,512]{1,0:T(8,128)S(1)}, f32[256,512]{1,0:T(8,128)S(1)}, u32[]{:S(2)}, u32[]{:S(2)}) collective-permute-start(f32[256,512]{1,0:T(8,128)S(1)} %add.295), channel_id=1, source_target_pairs={{0,16},{4,12},{8,24},{12,4},{16,0},{20,28},{24,8},{28,20},{1,17},{... | collective-permute-start | bytes 1572872 | tf_op jit(solution)/shard_map/ppermute | solution.py:329
  118.5 2.1 %collective-permute-start.15 = (f32[296,512]{1,0:T(8,128)}, f32[296,512]{1,0:T(8,128)}, u32[]{:S(2)}, u32[]{:S(2)}) collective-permute-start(f32[296,512]{1,0:T(8,128)} %collective-permute-done.13.refs_11_), channel_id=1, source_target_pairs={{2,1},{6,5},{10,9},{14,13},{18,17},{22,21},{26,25},{30,29}} | collective-permute-start | bytes 1818632 | tf_op jit(solution)/shard_map/ppermute | solution.py:346
  120.6 2.5 %collective-permute-start.16 = (f32[296,512]{1,0:T(8,128)}, f32[296,512]{1,0:T(8,128)}, u32[]{:S(2)}, u32[]{:S(2)}) collective-permute-start(f32[296,512]{1,0:T(8,128)} %collective-permute-done.13.refs_11_), channel_id=1, source_target_pairs={{2,3},{6,7},{10,11},{14,15},{18,19},{22,23},{26,27},{30,31}} | collective-permute-start | bytes 1818632 | tf_op jit(solution)/shard_map/ppermute | solution.py:350
  123.2 2.2 %collective-permute-done.22 = f32[256,512]{1,0:T(8,128)S(1)} collective-permute-done((f32[256,512]{1,0:T(8,128)S(1)}, f32[256,512]{1,0:T(8,128)S(1)}, u32[]{:S(2)}, u32[]{:S(2)}) %collective-permute-start.22) | collective-permute-done | bytes 524320 | tf_op jit(solution)/shard_map/ppermute | solution.py:329
  125.4 0.9 add.296.tm_ref
  126.3 4.5 %collective-permute-start.23 = (f32[256,512]{1,0:T(8,128)}, f32[256,512]{1,0:T(8,128)}, u32[]{:S(2)}, u32[]{:S(2)}) collective-permute-start(f32[256,512]{1,0:T(8,128)} %add.296.tm_ref), channel_id=1, source_target_pairs={{0,4},{4,0},{8,12},{12,8},{16,20},{20,16},{24,28},{28,24},{1,5},{5... | collective-permute-start | bytes 1572872 | tf_op jit(solution)/shard_map/ppermute | solution.py:319
  130.7 0.6 convert_reduce_fusion.4
  132.6 0.7 reduce_max.9
  134.0 2.1 %collective-permute-start.24 = (f32[296,512]{1,0:T(8,128)}, f32[296,512]{1,0:T(8,128)}, u32[]{:S(2)}, u32[]{:S(2)}) collective-permute-start(f32[296,512]{1,0:T(8,128)} %copy-done.14), channel_id=1, source_target_pairs={{2,1},{6,5},{10,9},{14,13},{18,17},{22,21},{26,25},{30,29}} | collective-permute-start | bytes 1818632 | tf_op jit(solution)/shard_map/ppermute | solution.py:346
  136.1 2.1 %collective-permute-start.25 = (f32[296,512]{1,0:T(8,128)}, f32[296,512]{1,0:T(8,128)}, u32[]{:S(2)}, u32[]{:S(2)}) collective-permute-start(f32[296,512]{1,0:T(8,128)} %copy-done.14), channel_id=1, source_target_pairs={{2,3},{6,7},{10,11},{14,15},{18,19},{22,23},{26,27},{30,31}} | collective-permute-start | bytes 1818632 | tf_op jit(solution)/shard_map/ppermute | solution.py:350
  138.3 9.3 %rows.1 = (bf16[1024,1024]{1,0:T(8,128)(2,1)S(1)}, bf16[1024,1024]{1,0:T(8,128)(2,1)S(1)}, f32[512,1024]{1,0:T(8,128)}) custom-call(s32[2]{0:T(128)} %pad_add_fusion.6.refs_6_.where_ref.refs_0_, f32[512,512]{1,0:T(8,128)S(1)} %get-tuple-element.368.panel_ref, f32[256,1536]{1,0:T(8,128)} %add.293.mine_ref, f32[256,1536]{1,0:T(8,128)} %collective-permute-done.19.mate_ref, ...), custom_call_target="tpu_custom_call" | custom-call | flops 10000000000 | bytes 1 | tf_op jit(solution)/shard_map/rows/pallas_call | solution.py:215
  147.5 1.4 collective-permute-done.24.refs_16_
  148.9 2.1 %collective-permute-done.25.refs_17_ = f32[296,512]{1,0:T(8,128)} collective-permute-done((f32[296,512]{1,0:T(8,128)}, f32[296,512]{1,0:T(8,128)}, u32[]{:S(2)}, u32[]{:S(2)}) %collective-permute-start.25) | collective-permute-done | bytes 606240 | tf_op jit(solution)/shard_map/ppermute | solution.py:350
  151.0 8.8 %finish.1 = f32[512,1024]{1,0:T(8,128)} custom-call(s32[2]{0:T(128)} %pad_add_fusion.6.refs_6_.where_ref.refs_0_, s32[80]{0:T(128)} %get-tuple-element.382.target_ref.refs_1_, s32[1]{0:T(128)} %bitcast.18.count_ref.refs_2_, f32[512,1024]{1,0:T(8,128)} %get-tuple-element.361.refs_3_, bf16[1024,1024]{1,0:T(8,128)(2,1)S(1)} %get-tuple-element.665.refs_4_, ...), custom_call_target="tpu_custom_call" | custom-call | flops 10000000000 | bytes 1 | tf_op jit(solution)/shard_map/finish/pallas_call | solution.py:281
  (88 shorter events, 7.8 us)
Async XLA Ops:
  0.0 11.8 %copy-start = (f32[512,1024]{1,0:T(8,128)S(1)}, f32[512,1024]{1,0:T(8,128)}, u32[]{:S(2)}) copy-start(f32[512,1024]{1,0:T(8,128)} %refs_2_.3) | copy-start | bytes 6291460
  0.0 8.7 %copy-start.10 = (s32[2,512]{1,0:T(2,128)S(1)}, s32[2,512]{1,0:T(2,128)}, u32[]{:S(2)}) copy-start(s32[2,512]{1,0:T(2,128)} %param.7) | copy-start | bytes 12292
  0.0 11.8 %collective-permute-start.6 = (f32[512,1024]{1,0:T(8,128)}, f32[512,1024]{1,0:T(8,128)}, u32[]{:S(2)}, u32[]{:S(2)}) collective-permute-start(f32[512,1024]{1,0:T(8,128)} %refs_2_.3), channel_id=1, source_target_pairs={{0,4},{4,0},{8,12},{12,8},{16,20},{20,16},{24,28},{28,24},{1,5},{5... | collective-permute-start | bytes 6291464 | tf_op jit(solution)/shard_map/ppermute | solution.py:319
  17.6 15.7 %collective-permute-start.7 = (f32[576,512]{1,0:T(8,128)}, f32[576,512]{1,0:T(8,128)S(1)}, u32[]{:S(2)}, u32[]{:S(2)}) collective-permute-start(f32[576,512]{1,0:T(8,128)} %pick.8), channel_id=1, source_target_pairs={{0,8},{4,20},{8,0},{12,28},{16,24},{20,4},{24,16},{28,12},{1,9},{5... | collective-permute-start | bytes 3538952 | tf_op jit(solution)/shard_map/ppermute | solution.py:329
  17.9 27.4 %collective-permute-start.9 = (f32[512,512]{1,0:T(8,128)}, f32[512,512]{1,0:T(8,128)}, u32[]{:S(2)}, u32[]{:S(2)}) collective-permute-start(f32[512,512]{1,0:T(8,128)} %fusion.39.refs_2_.one_ref.refs_6_), channel_id=1, source_target_pairs={{0,2},{4,6},{8,10},{12,14},{16,18},{20,22},{24,26},{28,30}} | collective-permute-start | bytes 3145736 | tf_op jit(solution)/shard_map/ppermute | solution.py:339
  34.9 15.7 %collective-permute-start.8 = (f32[576,512]{1,0:T(8,128)S(1)}, f32[576,512]{1,0:T(8,128)}, u32[]{:S(2)}, u32[]{:S(2)}) collective-permute-start(f32[576,512]{1,0:T(8,128)S(1)} %add.289), channel_id=1, source_target_pairs={{0,16},{4,12},{8,24},{12,4},{16,0},{20,28},{24,8},{28,20},{1,17},{... | collective-permute-start | bytes 3538952 | tf_op jit(solution)/shard_map/ppermute | solution.py:329
  45.3 23.1 %collective-permute-start.10 = (f32[512,512]{1,0:T(8,128)}, f32[512,512]{1,0:T(8,128)}, u32[]{:S(2)}, u32[]{:S(2)}) collective-permute-start(f32[512,512]{1,0:T(8,128)} %collective-permute-done.9.refs_3_.refs_7_), channel_id=1, source_target_pairs={{2,1},{6,5},{10,9},{14,13},{18,17},{22,21},{26,25},{30,29}} | collective-permute-start | bytes 3145736 | tf_op jit(solution)/shard_map/ppermute | solution.py:346
  47.7 23.0 %collective-permute-start.11 = (f32[512,512]{1,0:T(8,128)}, f32[512,512]{1,0:T(8,128)}, u32[]{:S(2)}, u32[]{:S(2)}) collective-permute-start(f32[512,512]{1,0:T(8,128)} %collective-permute-done.9.refs_3_.refs_7_), channel_id=1, source_target_pairs={{2,3},{6,7},{10,11},{14,15},{18,19},{22,23},{26,27},{30,31}} | collective-permute-start | bytes 3145736 | tf_op jit(solution)/shard_map/ppermute | solution.py:350
  52.1 7.9 %copy-start.8 = (f32[576,512]{1,0:T(8,128)}, f32[576,512]{1,0:T(8,128)S(1)}, u32[]{:S(2)}) copy-start(f32[576,512]{1,0:T(8,128)S(1)} %add.290.mine_ref) | copy-start | bytes 3538948
  52.1 24.2 %collective-permute-start.12 = (f32[576,512]{1,0:T(8,128)S(1)}, f32[576,512]{1,0:T(8,128)S(1)}, u32[]{:S(2)}, u32[]{:S(2)}) collective-permute-start(f32[576,512]{1,0:T(8,128)S(1)} %add.290.mine_ref), channel_id=1, source_target_pairs={{0,4},{4,0},{8,12},{12,8},{16,20},{20,16},{24,28},{28,24},{1,5},{5... | collective-permute-start | bytes 3538952 | tf_op jit(solution)/shard_map/ppermute | solution.py:319
  60.1 25.4 %collective-permute-start.14 = (f32[256,1536]{1,0:T(8,128)}, f32[256,1536]{1,0:T(8,128)}, u32[]{:S(2)}, u32[]{:S(2)}) collective-permute-start(f32[256,1536]{1,0:T(8,128)} %pick.10), channel_id=1, source_target_pairs={{0,8},{4,20},{8,0},{12,28},{16,24},{20,4},{24,16},{28,12},{1,9},{5... | collective-permute-start | bytes 4718600 | tf_op jit(solution)/shard_map/ppermute | solution.py:329
  70.7 6.7 %copy-start.1 = (f32[2,512,512]{2,1,0:T(8,128)S(1)}, f32[2,512,512]{2,1,0:T(8,128)}, u32[]{:S(2)}) copy-start(f32[2,512,512]{2,1,0:T(8,128)} %u_ref.1) | copy-start | bytes 6291460
  76.4 1.1 copy-start.11
  77.4 8.1 %copy-start.7 = (f32[256,1536]{1,0:T(8,128)S(1)}, f32[256,1536]{1,0:T(8,128)}, u32[]{:S(2)}) copy-start(f32[256,1536]{1,0:T(8,128)} %pick.10) | copy-start | bytes 4718596
  85.5 1.9 %copy-start.13 = (f32[296,512]{1,0:T(8,128)S(1)}, f32[296,512]{1,0:T(8,128)}, u32[]{:S(2)}) copy-start(f32[296,512]{1,0:T(8,128)} %get-tuple-element.369.refs_14_) | copy-start | bytes 1818628
  85.5 3.2 %copy-start.15 = (f32[256,512]{1,0:T(8,128)S(1)}, f32[256,512]{1,0:T(8,128)}, u32[]{:S(2)}) copy-start(f32[256,512]{1,0:T(8,128)} %get-tuple-element.372) | copy-start | bytes 1572868
  85.5 7.1 %copy-start.12 = (f32[296,512]{1,0:T(8,128)S(1)}, f32[296,512]{1,0:T(8,128)}, u32[]{:S(2)}) copy-start(f32[296,512]{1,0:T(8,128)} %get-tuple-element.363.refs_10_) | copy-start | bytes 1818628
  85.5 8.6 %copy-start.9 = (f32[256,512]{1,0:T(8,128)S(1)}, f32[256,512]{1,0:T(8,128)}, u32[]{:S(2)}) copy-start(f32[256,512]{1,0:T(8,128)} %get-tuple-element.371) | copy-start | bytes 1572868
  87.3 25.4 %collective-permute-start.18 = (f32[256,1536]{1,0:T(8,128)S(1)}, f32[256,1536]{1,0:T(8,128)S(1)}, u32[]{:S(2)}, u32[]{:S(2)}) collective-permute-start(f32[256,1536]{1,0:T(8,128)S(1)} %add.292), channel_id=1, source_target_pairs={{0,16},{4,12},{8,24},{12,4},{16,0},{20,28},{24,8},{28,20},{1,17},{... | collective-permute-start | bytes 4718600 | tf_op jit(solution)/shard_map/ppermute | solution.py:329
  87.3 14.1 %collective-permute-start.17 = (f32[296,512]{1,0:T(8,128)S(1)}, f32[296,512]{1,0:T(8,128)S(1)}, u32[]{:S(2)}, u32[]{:S(2)}) collective-permute-start(f32[296,512]{1,0:T(8,128)S(1)} %copy-done.13), channel_id=1, source_target_pairs={{0,2},{4,6},{8,10},{12,14},{16,18},{20,22},{24,26},{28,30}} | collective-permute-start | bytes 1818632 | tf_op jit(solution)/shard_map/ppermute | solution.py:339
  88.7 5.4 %collective-permute-start.20 = (f32[256,512]{1,0:T(8,128)S(1)}, f32[256,512]{1,0:T(8,128)S(1)}, u32[]{:S(2)}, u32[]{:S(2)}) collective-permute-start(f32[256,512]{1,0:T(8,128)S(1)} %copy-done.15), channel_id=1, source_target_pairs={{0,4},{4,0},{8,12},{12,8},{16,20},{20,16},{24,28},{28,24},{1,5},{5... | collective-permute-start | bytes 1572872 | tf_op jit(solution)/shard_map/ppermute | solution.py:319
  92.6 24.0 %collective-permute-start.13 = (f32[296,512]{1,0:T(8,128)S(1)}, f32[296,512]{1,0:T(8,128)}, u32[]{:S(2)}, u32[]{:S(2)}) collective-permute-start(f32[296,512]{1,0:T(8,128)S(1)} %copy-done.12), channel_id=1, source_target_pairs={{0,2},{4,6},{8,10},{12,14},{16,18},{20,22},{24,26},{28,30}} | collective-permute-start | bytes 1818632 | tf_op jit(solution)/shard_map/ppermute | solution.py:339
  94.2 22.4 %collective-permute-start.21 = (f32[256,512]{1,0:T(8,128)S(1)}, f32[256,512]{1,0:T(8,128)S(1)}, u32[]{:S(2)}, u32[]{:S(2)}) collective-permute-start(f32[256,512]{1,0:T(8,128)S(1)} %add.294), channel_id=1, source_target_pairs={{0,8},{4,20},{8,0},{12,28},{16,24},{20,4},{24,16},{28,12},{1,9},{5... | collective-permute-start | bytes 1572872 | tf_op jit(solution)/shard_map/ppermute | solution.py:329
  101.5 0.8 copy-start.14
  113.9 24.3 %collective-permute-start.19 = (f32[256,1536]{1,0:T(8,128)}, f32[256,1536]{1,0:T(8,128)}, u32[]{:S(2)}, u32[]{:S(2)}) collective-permute-start(f32[256,1536]{1,0:T(8,128)} %add.293.mine_ref), channel_id=1, source_target_pairs={{0,4},{4,0},{8,12},{12,8},{16,20},{20,16},{24,28},{28,24},{1,5},{5... | collective-permute-start | bytes 4718600 | tf_op jit(solution)/shard_map/ppermute | solution.py:319
  116.6 8.8 %collective-permute-start.22 = (f32[256,512]{1,0:T(8,128)S(1)}, f32[256,512]{1,0:T(8,128)S(1)}, u32[]{:S(2)}, u32[]{:S(2)}) collective-permute-start(f32[256,512]{1,0:T(8,128)S(1)} %add.295), channel_id=1, source_target_pairs={{0,16},{4,12},{8,24},{12,4},{16,0},{20,28},{24,8},{28,20},{1,17},{... | collective-permute-start | bytes 1572872 | tf_op jit(solution)/shard_map/ppermute | solution.py:329
  118.5 17.6 %collective-permute-start.15 = (f32[296,512]{1,0:T(8,128)}, f32[296,512]{1,0:T(8,128)}, u32[]{:S(2)}, u32[]{:S(2)}) collective-permute-start(f32[296,512]{1,0:T(8,128)} %collective-permute-done.13.refs_11_), channel_id=1, source_target_pairs={{2,1},{6,5},{10,9},{14,13},{18,17},{22,21},{26,25},{30,29}} | collective-permute-start | bytes 1818632 | tf_op jit(solution)/shard_map/ppermute | solution.py:346
  120.6 17.6 %collective-permute-start.16 = (f32[296,512]{1,0:T(8,128)}, f32[296,512]{1,0:T(8,128)}, u32[]{:S(2)}, u32[]{:S(2)}) collective-permute-start(f32[296,512]{1,0:T(8,128)} %collective-permute-done.13.refs_11_), channel_id=1, source_target_pairs={{2,3},{6,7},{10,11},{14,15},{18,19},{22,23},{26,27},{30,31}} | collective-permute-start | bytes 1818632 | tf_op jit(solution)/shard_map/ppermute | solution.py:350
  126.3 12.0 %collective-permute-start.23 = (f32[256,512]{1,0:T(8,128)}, f32[256,512]{1,0:T(8,128)}, u32[]{:S(2)}, u32[]{:S(2)}) collective-permute-start(f32[256,512]{1,0:T(8,128)} %add.296.tm_ref), channel_id=1, source_target_pairs={{0,4},{4,0},{8,12},{12,8},{16,20},{20,16},{24,28},{28,24},{1,5},{5... | collective-permute-start | bytes 1572872 | tf_op jit(solution)/shard_map/ppermute | solution.py:319
  134.0 14.9 %collective-permute-start.24 = (f32[296,512]{1,0:T(8,128)}, f32[296,512]{1,0:T(8,128)}, u32[]{:S(2)}, u32[]{:S(2)}) collective-permute-start(f32[296,512]{1,0:T(8,128)} %copy-done.14), channel_id=1, source_target_pairs={{2,1},{6,5},{10,9},{14,13},{18,17},{22,21},{26,25},{30,29}} | collective-permute-start | bytes 1818632 | tf_op jit(solution)/shard_map/ppermute | solution.py:346
  136.1 14.9 %collective-permute-start.25 = (f32[296,512]{1,0:T(8,128)}, f32[296,512]{1,0:T(8,128)}, u32[]{:S(2)}, u32[]{:S(2)}) collective-permute-start(f32[296,512]{1,0:T(8,128)} %copy-done.14), channel_id=1, source_target_pairs={{2,3},{6,7},{10,11},{14,15},{18,19},{22,23},{26,27},{30,31}} | collective-permute-start | bytes 1818632 | tf_op jit(solution)/shard_map/ppermute | solution.py:350
  147.5 12.3 %copy-start.3 = (bf16[1024,1024]{1,0:T(8,128)(2,1)}, bf16[1024,1024]{1,0:T(8,128)(2,1)S(1)}, u32[]{:S(2)}) copy-start(bf16[1024,1024]{1,0:T(8,128)(2,1)S(1)} %get-tuple-element.665.refs_4_) | copy-start | bytes 6291460
  147.5 12.3 %copy-start.4 = (bf16[1024,1024]{1,0:T(8,128)(2,1)}, bf16[1024,1024]{1,0:T(8,128)(2,1)S(1)}, u32[]{:S(2)}) copy-start(bf16[1024,1024]{1,0:T(8,128)(2,1)S(1)} %get-tuple-element.666.refs_5_) | copy-start | bytes 6291460

commit v2 on v1

--- a/solution.py
+++ b/solution.py
@@ -7,6 +7,8 @@
 
 BATCH = 320
 SHARE = 80
+GROUP = 8
+UPPER = 296
 F32, BF16 = jnp.float32, jnp.bfloat16
 SMEM, VMEM, ANY = (pl.BlockSpec(memory_space=space) for space in (pltpu.SMEM, pltpu.VMEM, pl.ANY))
 COSTS = dict(middle=6000000000, rows=10000000000, finish=10000000000, place=1)
@@ -77,14 +79,16 @@
         for index_ref, vector, segments in zip(index_refs, lists, pieces):
 
             def step(i, carry):
-                wanted = index_ref[i]
-                at = pl.ds(jnp.maximum(wanted, 0), 1)
+                start = i * GROUP
+                wanted = [index_ref[start + k] for k in range(GROUP)]
                 for output, source, row, column, width in segments:
-                    value = jnp.where(wanted >= 0, chip[at, source : source + width], 0.0)
-                    out_refs[output][pl.ds(row + i, 1), column : column + width] = value
+                    values = [chip[pl.ds(jnp.maximum(w, 0), 1), source : source + width] for w in wanted]
+                    values = [jnp.where(w >= 0, v, 0.0) for w, v in zip(wanted, values)]
+                    for k, value in enumerate(values):
+                        out_refs[output][pl.ds(row + start + k, 1), column : column + width] = value
                 return carry
 
-            lax.fori_loop(0, vector.shape[0], step, 0, unroll=8)
+            lax.fori_loop(0, vector.shape[0] // GROUP, step, 0)
 
     return pl.pallas_call(
         body,
@@ -105,14 +109,68 @@
     return found
 
 
-def middle_step(matrix, one, mine, mate, lower, upper, core, slots, targets, count, size):
+def top_step(ones, wanted, where, held):
+    rows, width = ones[0].shape
+    half = wanted.shape[0] // 2
+    many = len(ones)
+
+    def body(*refs):
+        where_ref, wanted_ref, one_refs = refs[0], refs[1], refs[2 : 2 + many]
+        keep_ref, give_ref, one, sem = refs[2 + many :]
+        for ref, places in zip(one_refs, held):
+
+            @pl.when(among(where_ref[1], places))
+            def _():
+                copy = pltpu.make_async_copy(ref, one, sem.at[0])
+                copy.start()
+                copy.wait()
+
+        high, rest = split(one[...])
+        low = (one[...] - high.astype(F32) - rest.astype(F32)).astype(BF16)
+        for k, ref in enumerate((keep_ref, give_ref)):
+            chosen = wanted_ref[k * half : (k + 1) * half, :] == lax.broadcasted_iota(jnp.int32, (half, rows), 1)
+            chosen = jnp.where(chosen, 1.0, 0.0).astype(BF16)
+            part = lambda x: jnp.dot(chosen, x, preferred_element_type=F32)
+            ref[...] = part(high) + (part(rest) + part(low))
+
+    shape = jax.ShapeDtypeStruct((half, width), F32)
+    return pl.pallas_call(
+        body,
+        out_shape=(shape, shape),
+        in_specs=[SMEM, VMEM] + [ANY] * many,
+        out_specs=(VMEM, VMEM),
+        scratch_shapes=[pltpu.VMEM((rows, width), F32), pltpu.SemaphoreType.DMA((1,))],
+        compiler_params=PARAMS,
+        cost_estimate=cost(6 * 10**9),
+        name="top",
+    )(where, wanted, *ones)
+
+
+def split_step(factors):
+    def body(factors_ref, high_ref, low_ref):
+        for k in range(factors.shape[0]):
+            high_ref[k], low_ref[k] = split(factors_ref[k])
+
+    shape = jax.ShapeDtypeStruct(factors.shape, BF16)
+    return pl.pallas_call(
+        body,
+        out_shape=(shape, shape),
+        in_specs=[VMEM],
+        out_specs=(VMEM, VMEM),
+        compiler_params=PARAMS,
+        cost_estimate=cost(6000000000),
+        name="split",
+    )(factors)
+
+
+def middle_step(matrix, one, mine, mate, lower_high, lower_low, upper, where, slots, targets, count, size):
     rows, cols = matrix.shape
-    width = lower.shape[1]
+    width = upper.shape[1]
     half = width // 2
     blocks = cols // width
-    part = (rows + SHARE) // 2
-
-    def body(core_ref, slot_ref, target_ref, count_ref, matrix_ref, one_ref, mine_ref, mate_ref, lower_ref, u_ref,
+    part = UPPER
+
+    def body(where_ref, slot_ref, target_ref, count_ref, matrix_ref, one_ref, mine_ref, mate_ref, lh_ref, ll_ref, u_ref,
              block_ref, upper_ref, under_ref, panel_ref, raw, pair, new_one):
         block_ref[...] = matrix_ref[...]
         raw[...] = jnp.zeros_like(raw)
@@ -129,51 +187,52 @@
             return carry
 
         lax.fori_loop(0, count_ref[0], bring, 0)
-        fresh = mul(split(raw[...]), split(u_ref[0]))
-        pair[pl.ds(rows, SHARE), :] = fresh
-        new_one[...] = one_ref[...]
-
-        def renew(i, carry):
-            new_one[pl.ds(target_ref[i], 1), :] = pair[pl.ds(rows + i, 1), :]
-            return carry
-
-        lax.fori_loop(0, count_ref[0], renew, 0)
-        first = pl.multiple_of(core_ref[0] * half, half)
-        second = pl.multiple_of(half - core_ref[0] * half, half)
-        panel = mul(split(lower_ref[0, :, pl.ds(first, half)]), split(mine_ref[:half, :])) + mul(
-            split(lower_ref[0, :, pl.ds(second, half)]), split(mate_ref[:half, :])
-        )
-        panel_ref[...] = panel
-        rest = block_ref[:, width : 2 * width] - mul(split(new_one[...]), split(panel))
-        pair[pl.ds(0, rows), :] = mul(split(rest), split(u_ref[1]))
-        upper_ref[...] = pair[:part, :]
-        under_ref[...] = pair[part:, :]
+        core = where_ref[0] % 2
+        first = pl.multiple_of(core * half, half)
+        second = pl.multiple_of(half - core * half, half)
+        lower = lambda start: (lh_ref[0, :, pl.ds(start, half)], ll_ref[0, :, pl.ds(start, half)])
+        panel_ref[...] = mul(lower(first), split(mine_ref[:half, :])) + mul(lower(second), split(mate_ref[:half, :]))
+
+        @pl.when(where_ref[1] == 0)
+        def _():
+            pair[pl.ds(rows, SHARE), :] = mul(split(raw[...]), split(u_ref[0]))
+            new_one[...] = one_ref[...]
+
+            def renew(i, carry):
+                new_one[pl.ds(target_ref[i], 1), :] = pair[pl.ds(rows + i, 1), :]
+                return carry
+
+            lax.fori_loop(0, count_ref[0], renew, 0)
+            rest = block_ref[:, width : 2 * width] - mul(split(new_one[...]), split(panel_ref[...]))
+            pair[pl.ds(0, rows), :] = mul(split(rest), split(u_ref[1]))
+            upper_ref[...] = pair[:part, :]
+            under_ref[...] = pair[part:, :]
 
     shape = lambda *s: jax.ShapeDtypeStruct(s, F32)
     return pl.pallas_call(
         body,
-        out_shape=(shape(rows, cols), shape(part, width), shape(part, width), shape(width, width)),
-        in_specs=[SMEM] * 4 + [VMEM] * 6,
+        out_shape=(shape(rows, cols), shape(part, width), shape(rows + SHARE - part, width), shape(width, width)),
+        in_specs=[SMEM] * 4 + [VMEM] * 7,
         out_specs=(VMEM,) * 4,
         scratch_shapes=[pltpu.VMEM(s, F32) for s in ((SHARE, width), (rows + SHARE, width), (rows, width))],
         compiler_params=PARAMS,
         cost_estimate=cost(COSTS["middle"]),
         name="middle",
-    )(core, slots, targets, count, matrix, one, mine, mate, lower, upper)
-
-
-def row_step(where, panel, mine, mate, top_mine, top_mate, lower, cols):
+    )(where, slots, targets, count, matrix, one, mine, mate, lower_high, lower_low, upper)
+
+
+def row_step(where, panel, mine, mate, top_mine, top_mate, lower_high, lower_low, cols):
     width = panel.shape[0]
     half = width // 2
     blocks = cols // width
     offset = cols - width
 
-    def body(where_ref, panel_ref, mine_ref, mate_ref, tm_ref, tt_ref, lower_ref, high_ref, low_ref, edge_ref, second):
+    def body(where_ref, panel_ref, mine_ref, mate_ref, tm_ref, tt_ref, lh_ref, ll_ref, high_ref, low_ref, edge_ref, second):
         me, first_column = where_ref[0], where_ref[1] == 0
         core = me % 2
         first = pl.multiple_of(core * half, half)
         other = pl.multiple_of(half - core * half, half)
-        lower = lambda k: (split(lower_ref[k, :, pl.ds(first, half)]), split(lower_ref[k, :, pl.ds(other, half)]))
+        lower = lambda k: tuple((lh_ref[k, :, pl.ds(at, half)], ll_ref[k, :, pl.ds(at, half)]) for at in (first, other))
         one, two = lower(0), lower(1)
         tops = (split(tm_ref[...]), split(tt_ref[...]))
         for b in range(blocks):
@@ -219,13 +278,13 @@
             jax.ShapeDtypeStruct((2 * width, cols), BF16),
             jax.ShapeDtypeStruct((width, cols), F32),
         ),
-        in_specs=[SMEM] + [VMEM] * 6,
+        in_specs=[SMEM] + [VMEM] * 7,
         out_specs=(VMEM,) * 3,
         scratch_shapes=[pltpu.VMEM((width, width), F32)],
         compiler_params=PARAMS,
         cost_estimate=cost(COSTS["rows"]),
         name="rows",
-    )(where, panel, mine, mate, top_mine, top_mate, lower)
+    )(where, panel, mine, mate, top_mine, top_mate, lower_high, lower_low)
 
 
 def finish_step(where, targets, count, block, ones, uppers, unders, high, low, edge, held):
@@ -233,12 +292,12 @@
     width = ones[0].shape[1]
     part = uppers[0].shape[0]
     parts = len(ones)
-    chunk = min(rows, 128)
+    chunk = width // 2
 
     def body(*refs):
         where_ref, target_ref, count_ref, block_ref, high_ref, low_ref = refs[:6]
         one_refs, upper_refs, under_refs = (refs[6 + parts * k : 6 + parts * (k + 1)] for k in range(3))
-        edge_ref, out_ref, one, pair, sems = refs[6 + 3 * parts :]
+        edge_ref, out_ref, one, pair, left_high, left_low, sems = refs[6 + 3 * parts :]
         me, column = where_ref[0], where_ref[1]
         first_column = column == 0
         for k in range(parts):
@@ -248,7 +307,7 @@
                 copies = [
                     pltpu.make_async_copy(one_refs[k], one, sems.at[0]),
                     pltpu.make_async_copy(upper_refs[k], pair.at[pl.ds(0, part)], sems.at[1]),
-                    pltpu.make_async_copy(under_refs[k], pair.at[pl.ds(part, part)], sems.at[2]),
+                    pltpu.make_async_copy(under_refs[k], pair.at[pl.ds(part, rows + SHARE - part)], sems.at[2]),
                 ]
                 for copy in copies:
                     copy.start()
@@ -269,14 +328,16 @@
 
             lax.fori_loop(0, count_ref[0], renew, 0)
 
-            @pl.loop(0, rows // chunk)
-            def _(c):
-                at = pl.ds(pl.multiple_of(c * chunk, chunk), chunk)
-                left = jnp.concatenate([one[at, :], pair[at, :]], axis=1)
-                total = block_ref[at, :] - mul(split(left), (high_ref[...], low_ref[...]))
-                out_ref[at, : 2 * width] = jnp.where(first_column, left, total[:, : 2 * width])
-                if cols > 2 * width:
-                    out_ref[at, 2 * width :] = total[:, 2 * width :]
+            for k, source in enumerate((one, pair)):
+                at = pl.ds(k * width, width)
+                left_high[:, at], left_low[:, at] = split(source[:rows, :])
+            for c in range(cols // chunk):
+                at = slice(c * chunk, (c + 1) * chunk)
+                total = block_ref[:, at] - mul((left_high[...], left_low[...]), (high_ref[:, at], low_ref[:, at]))
+                if c * chunk < 2 * width:
+                    held_here = (one if c * chunk < width else pair)[:rows, (c * chunk) % width : (c * chunk) % width + chunk]
+                    total = jnp.where(first_column, held_here, total)
+                out_ref[:, at] = total
 
     return pl.pallas_call(
         body,
@@ -286,6 +347,8 @@
         scratch_shapes=[
             pltpu.VMEM((rows, width), F32),
             pltpu.VMEM((rows + SHARE, width), F32),
+            pltpu.VMEM((rows, 2 * width), BF16),
+            pltpu.VMEM((rows, 2 * width), BF16),
             pltpu.SemaphoreType.DMA((3,)),
         ],
         compiler_params=PARAMS,
@@ -451,21 +514,19 @@
         [(0, 0, 0, 0, width)] + ([(0, 2 * width, 0, width, cols - 2 * width)] if blocks > 2 else []),
         [(0, 0, 0, cols - width, cols)],
     ]
-    (rest,) = pick([matrix, mate], [after(near, mine, hop), far], segments, [(half, 2 * cols - width)], work=6000000000)
+    (rest,) = pick([matrix, mate], [after(near, mine), far], segments, [(half, 2 * cols - width)], work=6000000000)
     ones = onward(column_one, hop)
     first, *others = axes_order()
     arriving = flip_axes(mine, first)
-    mine = mine + arriving
+    lowers = split_step(after(lower_inv, hop))
+    mine = after(mine, lowers[0]) + arriving
     mine, mates = gather_sum(mine, others)
 
     wanted = second_rows - me * rows
-    wanted = jnp.where((wanted >= 0) & (wanted < rows), wanted, -1)
     keep, give = jnp.where(core == 0, wanted[:half], wanted[half:]), jnp.where(core == 0, wanted[half:], wanted[:half])
-    top, given = pick(
-        ones, [after(keep, mine), give], [[(0, 0, 0, 0, width)], [(1, 0, 0, 0, width)]], [(half, width)] * 2, (where, held), 6000000000
-    )
+    top, given = top_step(ones, jnp.concatenate([after(keep, mine), give])[:, None], where, held)
     block, upper, under, panel = middle_step(
-        matrix, after(column_one, top), mine, mates, lower_inv, upper_inv, core[None], own_slot, own_row, count, size
+        matrix, after(column_one, top), mine, mates, *lowers, upper_inv, where, own_slot, own_row, count, size
     )
     hops = first_hop(upper), first_hop(under)
     given = swap_cores(given)
@@ -473,17 +534,18 @@
     rest = after(rest, mine)
     arriving = flip_axes(rest, first)
     rest = after(rest, upper) + arriving
-    uppers = onward(upper, after(hops[0], rest))
+    uppers = onward(upper, hops[0])
+    unders = onward(under, hops[1])
     arriving = flip_axes(top, first)
-    top = after(top, hops[0]) + arriving
-    unders = onward(under, after(hops[1], top))
+    top = after(top, upper, hops[1]) + arriving
     for pair in others:
         arriving = flip_axes(rest, pair)
-        rest = after(rest, hops[1]) + arriving
-        top = top + flip_axes(top, pair)
+        over = flip_axes(top, pair)
+        rest = after(rest, upper, hops[0]) + arriving
+        top = after(top, upper) + over
     rest_mine, rest_mates = rest, swap_cores(rest)
     top_mine, top_mate = top, swap_cores(top)
-    high, low, edge = row_step(where, after(panel, *uppers[1:]), rest_mine, rest_mates, top_mine, top_mate, lower_inv, cols)
+    high, low, edge = row_step(where, after(panel, *uppers[1:]), rest_mine, rest_mates, top_mine, top_mate, *lowers, cols)
     result = finish_step(where, own_row, count, block, ones, uppers, unders, high, low, edge, held)
 
     crowded = (moved > BATCH) | (jnp.max(shares) > SHARE)

time: 163 us -> 157 us (0.963)
  starting transfers between devices: 34 us -> 29.3 us
  waiting for transfers between devices: 53.9 us -> 55.7 us
    ppermute x3, waiting for transfers between devices: 15.5 us -> 26.3 us  [first_hop(): return lax.ppermute(x, 'pcol', [(0, 2)])]
    pallas_call x0 -> x2, Pallas kernels: none -> 7.45 us  [the longest x1 4.3 us: top_step(): pl.pallas_call(body, out_shape=(shape, shape), in_specs=[SMEM, VMEM] + [A...]
    ppermute x5, starting transfers between devices: 13.2 us -> 7.46 us  [swap_cores(): lax.ppermute(x, 'prow', [(i, i ^ 1) for i in range(lax.axis_size('prow'))])]
    pallas_call x3 -> x2, Pallas kernels: 17.8 us -> 12 us  [pick(): pl.pallas_call(body, out_shape=[jax.ShapeDtypeStruct(shape, F32) for shap...]
    ppermute x3, waiting for transfers between devices: 6.96 us -> 1.52 us  [onward(): parts += [current, lax.ppermute(current, 'pcol', [(even, even - 1)])]]
    ppermute x3, waiting for transfers between devices: 4.46 us -> 1.99 us  [onward(): parts.append(lax.ppermute(current, 'pcol', [(even, even + 1)]))]
    pallas_call x1, Pallas kernels: 8.02 us -> 6.17 us  [middle_step(): pl.pallas_call(body, out_shape=(shape(rows, cols), shape(part, width), sh...]
  transfers between devices with their start and end apart: 20 -> 20, of which waited for: 10 -> 10; matrix products, arithmetic and copies ran while one was open for 14% -> 12% of each run, Pallas kernels for 18% -> 23%
where the time goes in v2:
time: 157 us; the launch traced here: 154 us
  waiting for transfers between devices  55.7 us (35%)
  Pallas kernels  43 us (27%)
  starting transfers between devices  29.3 us (19%)
  other arithmetic  18 us (11%)
  between operations  2.98 us (2%)
  local copies, waits for them, and re-layouts  2.71 us (2%)
  matrix products  2.54 us (2%)
    ppermute x3, waiting for transfers between devices, first_hop(): return lax.ppermute(x, 'pcol', [(0, 2)])  26.3 us
    ppermute x6, waiting for transfers between devices, flip_axes(): lax.ppermute(x, 'prow', [(i, i ^ (second if i % 2 else first)) for i in r...  25.6 us
    pallas_call x2, Pallas kernels, pick(): pl.pallas_call(body, out_shape=[jax.ShapeDtypeStruct(shape, F32) for shap...  12 us
    pallas_call x1, Pallas kernels, row_step(): pl.pallas_call(body, out_shape=(jax.ShapeDtypeStruct((2 * width, cols), B...  9.13 us
    pallas_call x1, Pallas kernels, finish_step(): pl.pallas_call(body, out_shape=jax.ShapeDtypeStruct((rows, cols), F32), i...  8.2 us
    ppermute x5, starting transfers between devices, swap_cores(): lax.ppermute(x, 'prow', [(i, i ^ 1) for i in range(lax.axis_size('prow'))])  7.46 us
    ppermute x3, starting transfers between devices, onward(): parts.append(lax.ppermute(current, 'pcol', [(even, even + 1)]))  6.56 us
    ppermute x3, starting transfers between devices, onward(): parts += [current, lax.ppermute(current, 'pcol', [(even, even - 1)])]  6.52 us
  transfers between devices with their start and end apart: 20, of which 10 were waited for; matrix products, arithmetic and copies ran while one was open for 12% of the time, Pallas kernels for 23%

profile of v2, /device:TPU:23, one launch (start us, length us, event | category | flops | bytes accessed | tf_op | source)
XLA Modules:
  0.0 154.2 jit_solution(1601542585944504568)
XLA Ops:
  0.0 0.7 collective-permute-start.6
  0.7 2.5 %fusion.39.refs_2_.one_ref.refs_6_ = f32[512,512]{1,0:T(8,128)S(1)} fusion(f32[2,512,512]{2,1,0:T(8,128)} %u_ref.1, f32[512,1024]{1,0:T(8,128)} %refs_2_.3), kind=kOutput, calls=%fused_computation.79 | convolution fusion | flops 805306368 | bytes 3145728 | tf_op jit(solution)/shard_map/dot_general | solution.py:33
  3.2 1.3 collective-permute-start.7
  9.0 0.6 and_select_fusion.7.refs_0_
  10.0 0.6 and_select_fusion.6.refs_1_
  10.7 5.8 %pick.7 = f32[576,512]{1,0:T(8,128)} custom-call(s32[256]{0:T(256)} %and_select_fusion.7.refs_0_, s32[160]{0:T(256)} %and_select_fusion.6.refs_1_, f32[512,1024]{1,0:T(8,128)S(1)} %copy-done, f32[512,1024]{1,0:T(8,128)} %collective-permute-done.6.refs_3_), custom_call_target="tpu_custom_call" | custom-call | flops 1 | bytes 1 | tf_op jit(solution)/shard_map/pick/pallas_call | solution.py:93
  16.8 0.7 fusion.63
  17.9 12.9 %collective-permute-done.7.refs_3_.refs_7_ = f32[512,512]{1,0:T(8,128)} collective-permute-done((f32[512,512]{1,0:T(8,128)S(1)}, f32[512,512]{1,0:T(8,128)}, u32[]{:S(2)}, u32[]{:S(2)}) %collective-permute-start.7) | collective-permute-done | bytes 1048608 | tf_op jit(solution)/shard_map/ppermute | solution.py:402
  30.7 3.1 %split.1 = (bf16[2,512,512]{2,1,0:T(8,128)(2,1)}, bf16[2,512,512]{2,1,0:T(8,128)(2,1)}) custom-call(f32[2,512,512]{2,1,0:T(8,128)} %factors_ref), custom_call_target="tpu_custom_call" | custom-call | flops 6000000000 | bytes 1 | tf_op jit(solution)/shard_map/split/pallas_call | solution.py:155
  33.9 1.5 add.289
  35.9 0.6 and_select_fusion.4.refs_1_
  36.6 2.3 %collective-permute-start.10 = (f32[512,512]{1,0:T(8,128)}, f32[512,512]{1,0:T(8,128)}, u32[]{:S(2)}, u32[]{:S(2)}) collective-permute-start(f32[512,512]{1,0:T(8,128)} %collective-permute-done.7.refs_3_.refs_7_), channel_id=1, source_target_pairs={{2,1},{6,5},{10,9},{14,13},{18,17},{22,21},{26,25},{30,29}} | collective-permute-start | bytes 3145736 | tf_op jit(solution)/shard_map/ppermute | solution.py:409
  38.8 2.3 %collective-permute-start.11 = (f32[512,512]{1,0:T(8,128)}, f32[512,512]{1,0:T(8,128)}, u32[]{:S(2)}, u32[]{:S(2)}) collective-permute-start(f32[512,512]{1,0:T(8,128)} %collective-permute-done.7.refs_3_.refs_7_), channel_id=1, source_target_pairs={{2,3},{6,7},{10,11},{14,15},{18,19},{22,23},{26,27},{30,31}} | collective-permute-start | bytes 3145736 | tf_op jit(solution)/shard_map/ppermute | solution.py:413
  41.1 0.8 select_reduce_fusion.6
  42.5 8.4 %collective-permute-done.9 = f32[576,512]{1,0:T(8,128)} collective-permute-done((f32[576,512]{1,0:T(8,128)S(1)}, f32[576,512]{1,0:T(8,128)}, u32[]{:S(2)}, u32[]{:S(2)}) %collective-permute-start.9) | collective-permute-done | bytes 1179680 | tf_op jit(solution)/shard_map/ppermute | solution.py:392
  50.9 2.6 %add.290.mine_ref = f32[576,512]{1,0:T(8,128)} add(f32[576,512]{1,0:T(8,128)S(1)} %add.289, f32[576,512]{1,0:T(8,128)} %collective-permute-done.9) | non-fusion elementwise | flops 294912 | bytes 3538944 | tf_op jit(solution)/shard_map/add | solution.py:397
  53.5 1.8 %collective-permute-start.12 = (f32[576,512]{1,0:T(8,128)}, f32[576,512]{1,0:T(8,128)S(1)}, u32[]{:S(2)}, u32[]{:S(2)}) collective-permute-start(f32[576,512]{1,0:T(8,128)} %add.290.mine_ref), channel_id=1, source_target_pairs={{0,4},{4,0},{8,12},{12,8},{16,20},{20,16},{24,28},{28,24},{1,5},{5... | collective-permute-start | bytes 3538952 | tf_op jit(solution)/shard_map/ppermute | solution.py:382
  55.4 6.2 %pick.8 = f32[256,1536]{1,0:T(8,128)} custom-call(s32[256]{0:T(256)} %and_select_fusion.7.refs_0_, s32[256]{0:T(256)} %and_select_fusion.4.refs_1_, f32[512,1024]{1,0:T(8,128)S(1)} %copy-done, f32[512,1024]{1,0:T(8,128)} %collective-permute-done.6.refs_3_), custom_call_target="tpu_custom_call" | custom-call | flops 6000000000 | bytes 1 | tf_op jit(solution)/shard_map/pick/pallas_call | solution.py:93
  61.9 0.6 pad_add_fusion.7.refs_0_.where_ref
  62.5 0.9 copy.6.refs_1_
  63.3 4.3 %top.1 = (f32[256,512]{1,0:T(8,128)}, f32[256,512]{1,0:T(8,128)}) custom-call(s32[2]{0:T(128)} %pad_add_fusion.7.refs_0_.where_ref, s32[512,1]{1,0:T(8,128)} %copy.6.refs_1_, f32[512,512]{1,0:T(8,128)} %copy-done.9, f32[512,512]{1,0:T(8,128)} %collective-permute-done.7.refs_3_.refs_7_, f32[512,512]{1,0:T(8,128)} %collective-permute-done.10.refs_4_.refs_8_, ...), custom_call_target="tpu_custom_call" | custom-call | flops 6000000000 | bytes 1 | tf_op jit(solution)/shard_map/top/pallas_call | solution.py:137
  67.7 1.0 copy-done.12
  68.7 6.2 %middle.1 = (f32[512,1024]{1,0:T(8,128)}, f32[296,512]{1,0:T(8,128)}, f32[296,512]{1,0:T(8,128)}, f32[512,512]{1,0:T(8,128)S(1)}) custom-call(s32[2]{0:T(128)} %pad_add_fusion.7.refs_0_.where_ref, s32[80]{0:T(128)} %get-tuple-element.387.slot_ref, s32[80]{0:T(128)} %get-tuple-element.388.target_ref.refs_1_, s32[1]{0:T(128)} %bitcast.18.count_ref.refs_2_, ...), custom_call_target="tpu_custom_call" | custom-call | flops 6000000000 | bytes 1 | tf_op jit(solution)/shard_map/middle/pallas_call | solution.py:212
  74.9 6.7 %collective-permute-done.16 = f32[256,1536]{1,0:T(8,128)} collective-permute-done((f32[256,1536]{1,0:T(8,128)}, f32[256,1536]{1,0:T(8,128)}, u32[]{:S(2)}, u32[]{:S(2)}) %collective-permute-start.16) | collective-permute-done | bytes 1572896 | tf_op jit(solution)/shard_map/ppermute | solution.py:392
  81.5 1.6 %add.292 = f32[256,1536]{1,0:T(8,128)S(1)} add(f32[256,1536]{1,0:T(8,128)S(1)} %copy-done.8, f32[256,1536]{1,0:T(8,128)} %collective-permute-done.16) | non-fusion elementwise | flops 393216 | bytes 4718592 | tf_op jit(solution)/shard_map/add | solution.py:536
  83.5 1.3 collective-permute-start.13
  84.8 1.2 collective-permute-start.19
  85.9 1.3 collective-permute-start.20
  87.6 1.3 collective-permute-start.21
  88.9 11.5 %collective-permute-done.13.refs_11_ = f32[296,512]{1,0:T(8,128)} collective-permute-done((f32[296,512]{1,0:T(8,128)S(1)}, f32[296,512]{1,0:T(8,128)}, u32[]{:S(2)}, u32[]{:S(2)}) %collective-permute-start.13) | collective-permute-done | bytes 606240 | tf_op jit(solution)/shard_map/ppermute | solution.py:402
  100.4 8.0 %collective-permute-done.17 = f32[256,1536]{1,0:T(8,128)S(1)} collective-permute-done((f32[256,1536]{1,0:T(8,128)S(1)}, f32[256,1536]{1,0:T(8,128)S(1)}, u32[]{:S(2)}, u32[]{:S(2)}) %collective-permute-start.17) | collective-permute-done | bytes 1572896 | tf_op jit(solution)/shard_map/ppermute | solution.py:392
  108.4 1.3 add.293.mine_ref
  109.7 1.7 %collective-permute-start.18 = (f32[256,1536]{1,0:T(8,128)}, f32[256,1536]{1,0:T(8,128)}, u32[]{:S(2)}, u32[]{:S(2)}) collective-permute-start(f32[256,1536]{1,0:T(8,128)} %add.293.mine_ref), channel_id=1, source_target_pairs={{0,4},{4,0},{8,12},{12,8},{16,20},{20,16},{24,28},{28,24},{1,5},{5... | collective-permute-start | bytes 4718600 | tf_op jit(solution)/shard_map/ppermute | solution.py:382
  111.4 1.9 %collective-permute-done.20.refs_15_ = f32[296,512]{1,0:T(8,128)S(1)} collective-permute-done((f32[296,512]{1,0:T(8,128)S(1)}, f32[296,512]{1,0:T(8,128)S(1)}, u32[]{:S(2)}, u32[]{:S(2)}) %collective-permute-start.20) | collective-permute-done | bytes 606240 | tf_op jit(solution)/shard_map/ppermute | solution.py:402
  113.4 2.3 %collective-permute-start.22 = (f32[256,512]{1,0:T(8,128)S(1)}, f32[256,512]{1,0:T(8,128)S(1)}, u32[]{:S(2)}, u32[]{:S(2)}) collective-permute-start(f32[256,512]{1,0:T(8,128)S(1)} %add.295), channel_id=1, source_target_pairs={{0,16},{4,12},{8,24},{12,4},{16,0},{20,28},{24,8},{28,20},{1,17},{... | collective-permute-start | bytes 1572872 | tf_op jit(solution)/shard_map/ppermute | solution.py:392
  115.7 2.1 %collective-permute-start.14 = (f32[296,512]{1,0:T(8,128)}, f32[296,512]{1,0:T(8,128)}, u32[]{:S(2)}, u32[]{:S(2)}) collective-permute-start(f32[296,512]{1,0:T(8,128)} %collective-permute-done.13.refs_11_), channel_id=1, source_target_pairs={{2,1},{6,5},{10,9},{14,13},{18,17},{22,21},{26,25},{30,29}} | collective-permute-start | bytes 1818632 | tf_op jit(solution)/shard_map/ppermute | solution.py:409
  117.9 2.1 %collective-permute-start.15 = (f32[296,512]{1,0:T(8,128)}, f32[296,512]{1,0:T(8,128)}, u32[]{:S(2)}, u32[]{:S(2)}) collective-permute-start(f32[296,512]{1,0:T(8,128)} %collective-permute-done.13.refs_11_), channel_id=1, source_target_pairs={{2,3},{6,7},{10,11},{14,15},{18,19},{22,23},{26,27},{30,31}} | collective-permute-start | bytes 1818632 | tf_op jit(solution)/shard_map/ppermute | solution.py:413
  120.0 2.6 %collective-permute-done.22 = f32[256,512]{1,0:T(8,128)S(1)} collective-permute-done((f32[256,512]{1,0:T(8,128)S(1)}, f32[256,512]{1,0:T(8,128)S(1)}, u32[]{:S(2)}, u32[]{:S(2)}) %collective-permute-start.22) | collective-permute-done | bytes 524320 | tf_op jit(solution)/shard_map/ppermute | solution.py:392
  122.6 0.9 add.296.tm_ref
  123.5 2.1 %collective-permute-start.23 = (f32[256,512]{1,0:T(8,128)}, f32[256,512]{1,0:T(8,128)}, u32[]{:S(2)}, u32[]{:S(2)}) collective-permute-start(f32[256,512]{1,0:T(8,128)} %add.296.tm_ref), channel_id=1, source_target_pairs={{0,4},{4,0},{8,12},{12,8},{16,20},{20,16},{24,28},{28,24},{1,5},{5... | collective-permute-start | bytes 1572872 | tf_op jit(solution)/shard_map/ppermute | solution.py:382
  125.5 0.7 convert_reduce_fusion.4
  127.0 0.6 reduce_max.9
  128.9 2.1 %collective-permute-start.24 = (f32[296,512]{1,0:T(8,128)}, f32[296,512]{1,0:T(8,128)}, u32[]{:S(2)}, u32[]{:S(2)}) collective-permute-start(f32[296,512]{1,0:T(8,128)} %copy-done.15), channel_id=1, source_target_pairs={{2,1},{6,5},{10,9},{14,13},{18,17},{22,21},{26,25},{30,29}} | collective-permute-start | bytes 1818632 | tf_op jit(solution)/shard_map/ppermute | solution.py:409
  131.0 2.1 %collective-permute-start.25 = (f32[296,512]{1,0:T(8,128)}, f32[296,512]{1,0:T(8,128)}, u32[]{:S(2)}, u32[]{:S(2)}) collective-permute-start(f32[296,512]{1,0:T(8,128)} %copy-done.15), channel_id=1, source_target_pairs={{2,3},{6,7},{10,11},{14,15},{18,19},{22,23},{26,27},{30,31}} | collective-permute-start | bytes 1818632 | tf_op jit(solution)/shard_map/ppermute | solution.py:413
  133.1 9.1 %rows.1 = (bf16[1024,1024]{1,0:T(8,128)(2,1)S(1)}, bf16[1024,1024]{1,0:T(8,128)(2,1)S(1)}, f32[512,1024]{1,0:T(8,128)}) custom-call(s32[2]{0:T(128)} %pad_add_fusion.7.refs_0_.where_ref, f32[512,512]{1,0:T(8,128)S(1)} %get-tuple-element.371.panel_ref, f32[256,1536]{1,0:T(8,128)} %add.293.mine_ref, f32[256,1536]{1,0:T(8,128)} %collective-permute-done.18.mate_ref, ...), custom_call_target="tpu_custom_call" | custom-call | flops 10000000000 | bytes 1 | tf_op jit(solution)/shard_map/rows/pallas_call | solution.py:274
  142.3 1.5 collective-permute-done.24.refs_16_
  143.8 2.0 %collective-permute-done.25.refs_17_ = f32[296,512]{1,0:T(8,128)} collective-permute-done((f32[296,512]{1,0:T(8,128)}, f32[296,512]{1,0:T(8,128)}, u32[]{:S(2)}, u32[]{:S(2)}) %collective-permute-start.25) | collective-permute-done | bytes 606240 | tf_op jit(solution)/shard_map/ppermute | solution.py:413
  145.8 8.2 %finish.1 = f32[512,1024]{1,0:T(8,128)} custom-call(s32[2]{0:T(128)} %pad_add_fusion.7.refs_0_.where_ref, s32[80]{0:T(128)} %get-tuple-element.388.target_ref.refs_1_, s32[1]{0:T(128)} %bitcast.18.count_ref.refs_2_, f32[512,1024]{1,0:T(8,128)} %get-tuple-element.368.refs_3_, bf16[1024,1024]{1,0:T(8,128)(2,1)S(1)} %get-tuple-element.671.refs_4_, ...), custom_call_target="tpu_custom_call" | custom-call | flops 10000000000 | bytes 1 | tf_op jit(solution)/shard_map/finish/pallas_call | solution.py:342
  (93 shorter events, 7.3 us)
Async XLA Ops:
  0.0 10.7 %copy-start = (f32[512,1024]{1,0:T(8,128)S(1)}, f32[512,1024]{1,0:T(8,128)}, u32[]{:S(2)}) copy-start(f32[512,1024]{1,0:T(8,128)} %refs_2_.3) | copy-start | bytes 6291460
  0.0 4.6 %copy-start.11 = (s32[2,512]{1,0:T(2,128)S(1)}, s32[2,512]{1,0:T(2,128)}, u32[]{:S(2)}) copy-start(s32[2,512]{1,0:T(2,128)} %param.7) | copy-start | bytes 12292
  0.0 10.7 %collective-permute-start.6 = (f32[512,1024]{1,0:T(8,128)}, f32[512,1024]{1,0:T(8,128)}, u32[]{:S(2)}, u32[]{:S(2)}) collective-permute-start(f32[512,1024]{1,0:T(8,128)} %refs_2_.3), channel_id=1, source_target_pairs={{0,4},{4,0},{8,12},{12,8},{16,20},{20,16},{24,28},{28,24},{1,5},{5... | collective-permute-start | bytes 6291464 | tf_op jit(solution)/shard_map/ppermute | solution.py:382
  3.2 13.3 %copy-start.9 = (f32[512,512]{1,0:T(8,128)}, f32[512,512]{1,0:T(8,128)S(1)}, u32[]{:S(2)}) copy-start(f32[512,512]{1,0:T(8,128)S(1)} %fusion.39.refs_2_.one_ref.refs_6_) | copy-start | bytes 3145732
  3.2 27.5 %collective-permute-start.7 = (f32[512,512]{1,0:T(8,128)S(1)}, f32[512,512]{1,0:T(8,128)}, u32[]{:S(2)}, u32[]{:S(2)}) collective-permute-start(f32[512,512]{1,0:T(8,128)S(1)} %fusion.39.refs_2_.one_ref.refs_6_), channel_id=1, source_target_pairs={{0,2},{4,6},{8,10},{12,14},{16,18},{20,22},{24,26},{28,30}} | collective-permute-start | bytes 3145736 | tf_op jit(solution)/shard_map/ppermute | solution.py:402
  16.5 17.4 %collective-permute-start.8 = (f32[576,512]{1,0:T(8,128)}, f32[576,512]{1,0:T(8,128)}, u32[]{:S(2)}, u32[]{:S(2)}) collective-permute-start(f32[576,512]{1,0:T(8,128)} %pick.7), channel_id=1, source_target_pairs={{0,8},{4,20},{8,0},{12,28},{16,24},{20,4},{24,16},{28,12},{1,9},{5... | collective-permute-start | bytes 3538952 | tf_op jit(solution)/shard_map/ppermute | solution.py:392
  17.9 16.0 %copy-start.7 = (f32[576,512]{1,0:T(8,128)S(1)}, f32[576,512]{1,0:T(8,128)}, u32[]{:S(2)}) copy-start(f32[576,512]{1,0:T(8,128)} %pick.7) | copy-start | bytes 3538948
  35.4 15.5 %collective-permute-start.9 = (f32[576,512]{1,0:T(8,128)S(1)}, f32[576,512]{1,0:T(8,128)}, u32[]{:S(2)}, u32[]{:S(2)}) collective-permute-start(f32[576,512]{1,0:T(8,128)S(1)} %add.289), channel_id=1, source_target_pairs={{0,16},{4,12},{8,24},{12,4},{16,0},{20,28},{24,8},{28,20},{1,17},{... | collective-permute-start | bytes 3538952 | tf_op jit(solution)/shard_map/ppermute | solution.py:392
  36.6 26.8 %collective-permute-start.10 = (f32[512,512]{1,0:T(8,128)}, f32[512,512]{1,0:T(8,128)}, u32[]{:S(2)}, u32[]{:S(2)}) collective-permute-start(f32[512,512]{1,0:T(8,128)} %collective-permute-done.7.refs_3_.refs_7_), channel_id=1, source_target_pairs={{2,1},{6,5},{10,9},{14,13},{18,17},{22,21},{26,25},{30,29}} | collective-permute-start | bytes 3145736 | tf_op jit(solution)/shard_map/ppermute | solution.py:409
  38.8 24.5 %collective-permute-start.11 = (f32[512,512]{1,0:T(8,128)}, f32[512,512]{1,0:T(8,128)}, u32[]{:S(2)}, u32[]{:S(2)}) collective-permute-start(f32[512,512]{1,0:T(8,128)} %collective-permute-done.7.refs_3_.refs_7_), channel_id=1, source_target_pairs={{2,3},{6,7},{10,11},{14,15},{18,19},{22,23},{26,27},{30,31}} | collective-permute-start | bytes 3145736 | tf_op jit(solution)/shard_map/ppermute | solution.py:413
  53.5 14.1 %collective-permute-start.12 = (f32[576,512]{1,0:T(8,128)}, f32[576,512]{1,0:T(8,128)S(1)}, u32[]{:S(2)}, u32[]{:S(2)}) collective-permute-start(f32[576,512]{1,0:T(8,128)} %add.290.mine_ref), channel_id=1, source_target_pairs={{0,4},{4,0},{8,12},{12,8},{16,20},{20,16},{24,28},{28,24},{1,5},{5... | collective-permute-start | bytes 3538952 | tf_op jit(solution)/shard_map/ppermute | solution.py:382
  61.6 19.9 %collective-permute-start.16 = (f32[256,1536]{1,0:T(8,128)}, f32[256,1536]{1,0:T(8,128)}, u32[]{:S(2)}, u32[]{:S(2)}) collective-permute-start(f32[256,1536]{1,0:T(8,128)} %pick.8), channel_id=1, source_target_pairs={{0,8},{4,20},{8,0},{12,28},{16,24},{20,4},{24,16},{28,12},{1,9},{5... | collective-permute-start | bytes 4718600 | tf_op jit(solution)/shard_map/ppermute | solution.py:392
  63.3 5.4 %copy-start.1 = (f32[2,512,512]{2,1,0:T(8,128)S(1)}, f32[2,512,512]{2,1,0:T(8,128)}, u32[]{:S(2)}) copy-start(f32[2,512,512]{2,1,0:T(8,128)} %u_ref.1) | copy-start | bytes 6291460
  67.7 1.0 copy-start.12
  68.7 12.8 %copy-start.8 = (f32[256,1536]{1,0:T(8,128)S(1)}, f32[256,1536]{1,0:T(8,128)}, u32[]{:S(2)}) copy-start(f32[256,1536]{1,0:T(8,128)} %pick.8) | copy-start | bytes 4718596
  74.9 8.6 %copy-start.13 = (f32[296,512]{1,0:T(8,128)S(1)}, f32[296,512]{1,0:T(8,128)}, u32[]{:S(2)}) copy-start(f32[296,512]{1,0:T(8,128)} %get-tuple-element.370.refs_10_) | copy-start | bytes 1818628
  74.9 9.9 %copy-start.16 = (f32[256,512]{1,0:T(8,128)S(1)}, f32[256,512]{1,0:T(8,128)}, u32[]{:S(2)}) copy-start(f32[256,512]{1,0:T(8,128)} %get-tuple-element.377) | copy-start | bytes 1572868
  74.9 11.1 %copy-start.14 = (f32[296,512]{1,0:T(8,128)S(1)}, f32[296,512]{1,0:T(8,128)}, u32[]{:S(2)}) copy-start(f32[296,512]{1,0:T(8,128)} %get-tuple-element.378.refs_14_) | copy-start | bytes 1818628
  74.9 12.6 %copy-start.10 = (f32[256,512]{1,0:T(8,128)S(1)}, f32[256,512]{1,0:T(8,128)}, u32[]{:S(2)}) copy-start(f32[256,512]{1,0:T(8,128)} %get-tuple-element.376) | copy-start | bytes 1572868
  83.1 25.2 %collective-permute-start.17 = (f32[256,1536]{1,0:T(8,128)S(1)}, f32[256,1536]{1,0:T(8,128)S(1)}, u32[]{:S(2)}, u32[]{:S(2)}) collective-permute-start(f32[256,1536]{1,0:T(8,128)S(1)} %add.292), channel_id=1, source_target_pairs={{0,16},{4,12},{8,24},{12,4},{16,0},{20,28},{24,8},{28,20},{1,17},{... | collective-permute-start | bytes 4718600 | tf_op jit(solution)/shard_map/ppermute | solution.py:392
  83.5 16.9 %collective-permute-start.13 = (f32[296,512]{1,0:T(8,128)S(1)}, f32[296,512]{1,0:T(8,128)}, u32[]{:S(2)}, u32[]{:S(2)}) collective-permute-start(f32[296,512]{1,0:T(8,128)S(1)} %copy-done.13), channel_id=1, source_target_pairs={{0,2},{4,6},{8,10},{12,14},{16,18},{20,22},{24,26},{28,30}} | collective-permute-start | bytes 1818632 | tf_op jit(solution)/shard_map/ppermute | solution.py:402
  84.8 2.7 %collective-permute-start.19 = (f32[256,512]{1,0:T(8,128)S(1)}, f32[256,512]{1,0:T(8,128)S(1)}, u32[]{:S(2)}, u32[]{:S(2)}) collective-permute-start(f32[256,512]{1,0:T(8,128)S(1)} %copy-done.16), channel_id=1, source_target_pairs={{0,4},{4,0},{8,12},{12,8},{16,20},{20,16},{24,28},{28,24},{1,5},{5... | collective-permute-start | bytes 1572872 | tf_op jit(solution)/shard_map/ppermute | solution.py:382
  85.9 27.4 %collective-permute-start.20 = (f32[296,512]{1,0:T(8,128)S(1)}, f32[296,512]{1,0:T(8,128)S(1)}, u32[]{:S(2)}, u32[]{:S(2)}) collective-permute-start(f32[296,512]{1,0:T(8,128)S(1)} %copy-done.14), channel_id=1, source_target_pairs={{0,2},{4,6},{8,10},{12,14},{16,18},{20,22},{24,26},{28,30}} | collective-permute-start | bytes 1818632 | tf_op jit(solution)/shard_map/ppermute | solution.py:402
  87.6 25.7 %collective-permute-start.21 = (f32[256,512]{1,0:T(8,128)S(1)}, f32[256,512]{1,0:T(8,128)S(1)}, u32[]{:S(2)}, u32[]{:S(2)}) collective-permute-start(f32[256,512]{1,0:T(8,128)S(1)} %add.294), channel_id=1, source_target_pairs={{0,8},{4,20},{8,0},{12,28},{16,24},{20,4},{24,16},{28,12},{1,9},{5... | collective-permute-start | bytes 1572872 | tf_op jit(solution)/shard_map/ppermute | solution.py:392
  109.7 23.4 %collective-permute-start.18 = (f32[256,1536]{1,0:T(8,128)}, f32[256,1536]{1,0:T(8,128)}, u32[]{:S(2)}, u32[]{:S(2)}) collective-permute-start(f32[256,1536]{1,0:T(8,128)} %add.293.mine_ref), channel_id=1, source_target_pairs={{0,4},{4,0},{8,12},{12,8},{16,20},{20,16},{24,28},{28,24},{1,5},{5... | collective-permute-start | bytes 4718600 | tf_op jit(solution)/shard_map/ppermute | solution.py:382
  113.3 10.2 %copy-start.15 = (f32[296,512]{1,0:T(8,128)}, f32[296,512]{1,0:T(8,128)S(1)}, u32[]{:S(2)}) copy-start(f32[296,512]{1,0:T(8,128)S(1)} %collective-permute-done.20.refs_15_) | copy-start | bytes 1818628
  113.4 9.2 %collective-permute-start.22 = (f32[256,512]{1,0:T(8,128)S(1)}, f32[256,512]{1,0:T(8,128)S(1)}, u32[]{:S(2)}, u32[]{:S(2)}) collective-permute-start(f32[256,512]{1,0:T(8,128)S(1)} %add.295), channel_id=1, source_target_pairs={{0,16},{4,12},{8,24},{12,4},{16,0},{20,28},{24,8},{28,20},{1,17},{... | collective-permute-start | bytes 1572872 | tf_op jit(solution)/shard_map/ppermute | solution.py:392
  115.7 15.3 %collective-permute-start.14 = (f32[296,512]{1,0:T(8,128)}, f32[296,512]{1,0:T(8,128)}, u32[]{:S(2)}, u32[]{:S(2)}) collective-permute-start(f32[296,512]{1,0:T(8,128)} %collective-permute-done.13.refs_11_), channel_id=1, source_target_pairs={{2,1},{6,5},{10,9},{14,13},{18,17},{22,21},{26,25},{30,29}} | collective-permute-start | bytes 1818632 | tf_op jit(solution)/shard_map/ppermute | solution.py:409
  117.9 15.2 %collective-permute-start.15 = (f32[296,512]{1,0:T(8,128)}, f32[296,512]{1,0:T(8,128)}, u32[]{:S(2)}, u32[]{:S(2)}) collective-permute-start(f32[296,512]{1,0:T(8,128)} %collective-permute-done.13.refs_11_), channel_id=1, source_target_pairs={{2,3},{6,7},{10,11},{14,15},{18,19},{22,23},{26,27},{30,31}} | collective-permute-start | bytes 1818632 | tf_op jit(solution)/shard_map/ppermute | solution.py:413
  123.5 9.7 %collective-permute-start.23 = (f32[256,512]{1,0:T(8,128)}, f32[256,512]{1,0:T(8,128)}, u32[]{:S(2)}, u32[]{:S(2)}) collective-permute-start(f32[256,512]{1,0:T(8,128)} %add.296.tm_ref), channel_id=1, source_target_pairs={{0,4},{4,0},{8,12},{12,8},{16,20},{20,16},{24,28},{28,24},{1,5},{5... | collective-permute-start | bytes 1572872 | tf_op jit(solution)/shard_map/ppermute | solution.py:382
  128.9 14.9 %collective-permute-start.24 = (f32[296,512]{1,0:T(8,128)}, f32[296,512]{1,0:T(8,128)}, u32[]{:S(2)}, u32[]{:S(2)}) collective-permute-start(f32[296,512]{1,0:T(8,128)} %copy-done.15), channel_id=1, source_target_pairs={{2,1},{6,5},{10,9},{14,13},{18,17},{22,21},{26,25},{30,29}} | collective-permute-start | bytes 1818632 | tf_op jit(solution)/shard_map/ppermute | solution.py:409
  131.0 14.8 %collective-permute-start.25 = (f32[296,512]{1,0:T(8,128)}, f32[296,512]{1,0:T(8,128)}, u32[]{:S(2)}, u32[]{:S(2)}) collective-permute-start(f32[296,512]{1,0:T(8,128)} %copy-done.15), channel_id=1, source_target_pairs={{2,3},{6,7},{10,11},{14,15},{18,19},{22,23},{26,27},{30,31}} | collective-permute-start | bytes 1818632 | tf_op jit(solution)/shard_map/ppermute | solution.py:413
  142.3 11.7 %copy-start.3 = (bf16[1024,1024]{1,0:T(8,128)(2,1)}, bf16[1024,1024]{1,0:T(8,128)(2,1)S(1)}, u32[]{:S(2)}) copy-start(bf16[1024,1024]{1,0:T(8,128)(2,1)S(1)} %get-tuple-element.671.refs_4_) | copy-start | bytes 6291460
  142.3 11.7 %copy-start.4 = (bf16[1024,1024]{1,0:T(8,128)(2,1)}, bf16[1024,1024]{1,0:T(8,128)(2,1)S(1)}, u32[]{:S(2)}) copy-start(bf16[1024,1024]{1,0:T(8,128)(2,1)S(1)} %get-tuple-element.672.refs_5_) | copy-start | bytes 6291460

commit v3 on v2

--- a/solution.py
+++ b/solution.py
@@ -5,8 +5,9 @@
 from jax.experimental.pallas import tpu as pltpu
 from jax.sharding import PartitionSpec as P
 
-BATCH = 320
-SHARE = 80
+BATCH = 304
+SHARE = 72
+SMALL = 64
 GROUP = 8
 UPPER = 296
 F32, BF16 = jnp.float32, jnp.bfloat16
@@ -526,7 +527,7 @@
     keep, give = jnp.where(core == 0, wanted[:half], wanted[half:]), jnp.where(core == 0, wanted[half:], wanted[:half])
     top, given = top_step(ones, jnp.concatenate([after(keep, mine), give])[:, None], where, held)
     block, upper, under, panel = middle_step(
-        matrix, after(column_one, top), mine, mates, *lowers, upper_inv, where, own_slot, own_row, count, size
+        matrix, column_one, mine, mates, *lowers, upper_inv, where, own_slot, own_row, count, size
     )
     hops = first_hop(upper), first_hop(under)
     given = swap_cores(given)
@@ -549,11 +550,11 @@
     result = finish_step(where, own_row, count, block, ones, uppers, unders, high, low, edge, held)
 
     crowded = (moved > BATCH) | (jnp.max(shares) > SHARE)
-    trips = jnp.where(crowded, (moved + SHARE - 1) // SHARE, 0)
+    trips = jnp.where(crowded, (moved + SMALL - 1) // SMALL, 0)
 
     def more(number, result):
-        origins, own_slot, own_row, count = batch(number * SHARE, SHARE)
-        rows_here = gather_sum(pick([matrix, mate], [origins], [[(0, 0, 0, 0, cols)]], [(SHARE // 2, cols)])[0])
+        origins, own_slot, own_row, count = batch(number * SMALL, SMALL)
+        rows_here = gather_sum(pick([matrix, mate], [origins], [[(0, 0, 0, 0, cols)]], [(SMALL // 2, cols)])[0])
         raw = jnp.take(jnp.concatenate(rows_here, axis=0), own_slot, axis=0)
         one = product(raw[:, :width], upper_inv[0])
         two = product(raw[:, width : 2 * width] - product(one, panel), upper_inv[1])

time: 157 us -> 154 us (0.981)
  waiting for transfers between devices: 55.7 us -> 52.1 us
    ppermute x3, waiting for transfers between devices: 26.3 us -> 19.5 us  [first_hop(): return lax.ppermute(x, 'pcol', [(0, 2)])]
    add x1, other arithmetic: 2.61 us -> 0.23 us  [gather_sum(): x = x + flip_axes(x, pair)]
    ppermute x3, waiting for transfers between devices: 1.52 us -> 3.84 us  [onward(): parts += [current, lax.ppermute(current, 'pcol', [(even, even - 1)])]]
    ppermute x3, waiting for transfers between devices: 1.99 us -> 4.29 us  [onward(): parts.append(lax.ppermute(current, 'pcol', [(even, even + 1)]))]
    ppermute x5, starting transfers between devices: 7.46 us -> 9.41 us  [swap_cores(): lax.ppermute(x, 'prow', [(i, i ^ 1) for i in range(lax.axis_size('prow'))])]
    add x1, other arithmetic: 1.34 us -> 3.22 us  [shards(): rest = after(rest, upper, hops[0]) + arriving]
    ppermute x6, waiting for transfers between devices: 25.6 us -> 23.9 us  [flip_axes(): lax.ppermute(x, 'prow', [(i, i ^ (second if i % 2 else first)) for i in r...]
  transfers between devices with their start and end apart: 20 -> 20, of which waited for: 10 -> 12; matrix products, arithmetic and copies ran while one was open for 12% -> 15% of each run, Pallas kernels for 23% -> 23%
where the time goes in v3:
time: 154 us; the launch traced here: 152 us
  waiting for transfers between devices  52.1 us (34%)
  Pallas kernels  43.1 us (28%)
  starting transfers between devices  30.7 us (20%)
  other arithmetic  18.6 us (12%)
  between operations  3 us (2%)
  matrix products  2.54 us (2%)
  local copies, waits for them, and re-layouts  1.67 us (1%)
    ppermute x6, waiting for transfers between devices, flip_axes(): lax.ppermute(x, 'prow', [(i, i ^ (second if i % 2 else first)) for i in r...  23.9 us
    ppermute x3, waiting for transfers between devices, first_hop(): return lax.ppermute(x, 'pcol', [(0, 2)])  19.5 us
    pallas_call x2, Pallas kernels, pick(): pl.pallas_call(body, out_shape=[jax.ShapeDtypeStruct(shape, F32) for shap...  12 us
    ppermute x5, starting transfers between devices, swap_cores(): lax.ppermute(x, 'prow', [(i, i ^ 1) for i in range(lax.axis_size('prow'))])  9.41 us
    pallas_call x1, Pallas kernels, row_step(): pl.pallas_call(body, out_shape=(jax.ShapeDtypeStruct((2 * width, cols), B...  9.12 us
    pallas_call x1, Pallas kernels, finish_step(): pl.pallas_call(body, out_shape=jax.ShapeDtypeStruct((rows, cols), F32), i...  8.16 us
    pallas_call x1, Pallas kernels, middle_step(): pl.pallas_call(body, out_shape=(shape(rows, cols), shape(part, width), sh...  6.66 us
    ppermute x3, starting transfers between devices, onward(): parts.append(lax.ppermute(current, 'pcol', [(even, even + 1)]))  6.54 us
  transfers between devices with their start and end apart: 20, of which 12 were waited for; matrix products, arithmetic and copies ran while one was open for 15% of the time, Pallas kernels for 23%

profile of v3, /device:TPU:23, one launch (start us, length us, event | category | flops | bytes accessed | tf_op | source)
XLA Modules:
  0.0 151.7 jit_solution(11401270680259863527)
XLA Ops:
  0.0 0.7 collective-permute-start.6
  0.7 2.5 %fusion.40.one_ref.refs_2_.refs_6_ = f32[512,512]{1,0:T(8,128)S(1)} fusion(f32[2,512,512]{2,1,0:T(8,128)} %u_ref.1, f32[512,1024]{1,0:T(8,128)} %refs_2_.3), kind=kOutput, calls=%fused_computation.81 | convolution fusion | flops 805306368 | bytes 3145728 | tf_op jit(solution)/shard_map/dot_general | solution.py:34
  3.2 1.3 collective-permute-start.7
  6.6 0.6 and_select_fusion.7.refs_0_
  10.0 0.7 and_select_fusion.6.refs_1_
  10.6 5.7 %pick.7 = f32[560,512]{1,0:T(8,128)} custom-call(s32[256]{0:T(256)} %and_select_fusion.7.refs_0_, s32[152]{0:T(256)} %and_select_fusion.6.refs_1_, f32[512,1024]{1,0:T(8,128)S(1)} %copy-done, f32[512,1024]{1,0:T(8,128)} %collective-permute-done.6.refs_3_), custom_call_target="tpu_custom_call" | custom-call | flops 1 | bytes 1 | tf_op jit(solution)/shard_map/pick/pallas_call | solution.py:94
  16.7 14.1 %collective-permute-done.7.refs_3_.refs_7_ = f32[512,512]{1,0:T(8,128)} collective-permute-done((f32[512,512]{1,0:T(8,128)S(1)}, f32[512,512]{1,0:T(8,128)}, u32[]{:S(2)}, u32[]{:S(2)}) %collective-permute-start.7) | collective-permute-done | bytes 1048608 | tf_op jit(solution)/shard_map/ppermute | solution.py:403
  30.7 3.1 %split.1 = (bf16[2,512,512]{2,1,0:T(8,128)(2,1)}, bf16[2,512,512]{2,1,0:T(8,128)(2,1)}) custom-call(f32[2,512,512]{2,1,0:T(8,128)} %factors_ref), custom_call_target="tpu_custom_call" | custom-call | flops 6000000000 | bytes 1 | tf_op jit(solution)/shard_map/split/pallas_call | solution.py:156
  34.4 0.6 and_select_fusion.4.refs_1_
  35.0 14.2 %collective-permute-done.9 = f32[560,512]{1,0:T(8,128)S(1)} collective-permute-done((f32[560,512]{1,0:T(8,128)S(1)}, f32[560,512]{1,0:T(8,128)S(1)}, u32[]{:S(2)}, u32[]{:S(2)}) %collective-permute-start.9) | collective-permute-done | bytes 1146912 | tf_op jit(solution)/shard_map/ppermute | solution.py:393
  49.4 1.9 %collective-permute-start.10 = (f32[560,512]{1,0:T(8,128)S(1)}, f32[560,512]{1,0:T(8,128)}, u32[]{:S(2)}, u32[]{:S(2)}) collective-permute-start(f32[560,512]{1,0:T(8,128)S(1)} %add.290.mine_ref), channel_id=1, source_target_pairs={{0,4},{4,0},{8,12},{12,8},{16,20},{20,16},{24,28},{28,24},{1,5},{5... | collective-permute-start | bytes 3440648 | tf_op jit(solution)/shard_map/ppermute | solution.py:383
  51.3 6.2 %pick.8 = f32[256,1536]{1,0:T(8,128)} custom-call(s32[256]{0:T(256)} %and_select_fusion.7.refs_0_, s32[256]{0:T(256)} %and_select_fusion.4.refs_1_, f32[512,1024]{1,0:T(8,128)S(1)} %copy-done, f32[512,1024]{1,0:T(8,128)} %collective-permute-done.6.refs_3_), custom_call_target="tpu_custom_call" | custom-call | flops 6000000000 | bytes 1 | tf_op jit(solution)/shard_map/pick/pallas_call | solution.py:94
  57.8 0.8 fusion.64
  59.7 0.6 pad_add_fusion.7.where_ref.refs_0_
  60.5 0.8 select_reduce_fusion.6
  61.3 2.3 %collective-permute-start.17 = (f32[512,512]{1,0:T(8,128)}, f32[512,512]{1,0:T(8,128)}, u32[]{:S(2)}, u32[]{:S(2)}) collective-permute-start(f32[512,512]{1,0:T(8,128)} %collective-permute-done.7.refs_3_.refs_7_), channel_id=1, source_target_pairs={{2,1},{6,5},{10,9},{14,13},{18,17},{22,21},{26,25},{30,29}} | collective-permute-start | bytes 3145736 | tf_op jit(solution)/shard_map/ppermute | solution.py:410
  63.6 2.3 %collective-permute-start.18 = (f32[512,512]{1,0:T(8,128)}, f32[512,512]{1,0:T(8,128)}, u32[]{:S(2)}, u32[]{:S(2)}) collective-permute-start(f32[512,512]{1,0:T(8,128)} %collective-permute-done.7.refs_3_.refs_7_), channel_id=1, source_target_pairs={{2,3},{6,7},{10,11},{14,15},{18,19},{22,23},{26,27},{30,31}} | collective-permute-start | bytes 3145736 | tf_op jit(solution)/shard_map/ppermute | solution.py:414
  65.9 6.7 %middle.1 = (f32[512,1024]{1,0:T(8,128)}, f32[296,512]{1,0:T(8,128)}, f32[288,512]{1,0:T(8,128)}, f32[512,512]{1,0:T(8,128)S(1)}) custom-call(s32[2]{0:T(128)} %pad_add_fusion.7.where_ref.refs_0_, s32[72]{0:T(128)} %get-tuple-element.385.slot_ref, s32[72]{0:T(128)} %get-tuple-element.386.target_ref.refs_1_, s32[1]{0:T(128)} %bitcast.18.count_ref.refs_2_, ...), custom_call_target="tpu_custom_call" | custom-call | flops 6000000000 | bytes 1 | tf_op jit(solution)/shard_map/middle/pallas_call | solution.py:213
  72.5 5.0 %collective-permute-done.14 = f32[256,1536]{1,0:T(8,128)} collective-permute-done((f32[256,1536]{1,0:T(8,128)}, f32[256,1536]{1,0:T(8,128)}, u32[]{:S(2)}, u32[]{:S(2)}) %collective-permute-start.14) | collective-permute-done | bytes 1572896 | tf_op jit(solution)/shard_map/ppermute | solution.py:393
  77.5 2.7 %add.292 = f32[256,1536]{1,0:T(8,128)} add(f32[256,1536]{1,0:T(8,128)S(1)} %copy-done.7, f32[256,1536]{1,0:T(8,128)} %collective-permute-done.14) | non-fusion elementwise | flops 393216 | bytes 4718592 | tf_op jit(solution)/shard_map/add | solution.py:537
  80.5 0.9 copy.6.refs_1_
  81.4 1.4 collective-permute-start.11
  82.8 2.6 %collective-permute-done.17.refs_4_.refs_8_ = f32[512,512]{1,0:T(8,128)} collective-permute-done((f32[512,512]{1,0:T(8,128)}, f32[512,512]{1,0:T(8,128)}, u32[]{:S(2)}, u32[]{:S(2)}) %collective-permute-start.17) | collective-permute-done | bytes 1048608 | tf_op jit(solution)/shard_map/ppermute | solution.py:410
  85.4 2.3 %collective-permute-done.18.refs_5_.refs_9_ = f32[512,512]{1,0:T(8,128)} collective-permute-done((f32[512,512]{1,0:T(8,128)}, f32[512,512]{1,0:T(8,128)}, u32[]{:S(2)}, u32[]{:S(2)}) %collective-permute-start.18) | collective-permute-done | bytes 1048608 | tf_op jit(solution)/shard_map/ppermute | solution.py:414
  87.7 4.1 %top.1 = (f32[256,512]{1,0:T(8,128)}, f32[256,512]{1,0:T(8,128)}) custom-call(s32[2]{0:T(128)} %pad_add_fusion.7.where_ref.refs_0_, s32[512,1]{1,0:T(8,128)} %copy.6.refs_1_, f32[512,512]{1,0:T(8,128)} %copy-done.9, f32[512,512]{1,0:T(8,128)} %collective-permute-done.7.refs_3_.refs_7_, f32[512,512]{1,0:T(8,128)} %collective-permute-done.17.refs_4_.refs_8_, ...), custom_call_target="tpu_custom_call" | custom-call | flops 6000000000 | bytes 1 | tf_op jit(solution)/shard_map/top/pallas_call | solution.py:138
  91.8 0.9 collective-permute-start.19
  92.7 1.3 collective-permute-start.20
  94.5 1.1 add.294
  95.6 0.8 collective-permute-start.21
  96.4 2.3 %collective-permute-done.11.refs_11_ = f32[296,512]{1,0:T(8,128)} collective-permute-done((f32[296,512]{1,0:T(8,128)}, f32[296,512]{1,0:T(8,128)}, u32[]{:S(2)}, u32[]{:S(2)}) %collective-permute-start.11) | collective-permute-done | bytes 606240 | tf_op jit(solution)/shard_map/ppermute | solution.py:403
  98.6 2.2 %collective-permute-done.15 = f32[256,1536]{1,0:T(8,128)} collective-permute-done((f32[256,1536]{1,0:T(8,128)}, f32[256,1536]{1,0:T(8,128)}, u32[]{:S(2)}, u32[]{:S(2)}) %collective-permute-start.15) | collective-permute-done | bytes 1572896 | tf_op jit(solution)/shard_map/ppermute | solution.py:393
  100.8 3.2 %add.293.mine_ref = f32[256,1536]{1,0:T(8,128)} add(f32[256,1536]{1,0:T(8,128)} %add.292, f32[256,1536]{1,0:T(8,128)} %collective-permute-done.15) | non-fusion elementwise | flops 393216 | bytes 4718592 | tf_op jit(solution)/shard_map/add | solution.py:545
  104.1 3.9 %collective-permute-start.16 = (f32[256,1536]{1,0:T(8,128)}, f32[256,1536]{1,0:T(8,128)}, u32[]{:S(2)}, u32[]{:S(2)}) collective-permute-start(f32[256,1536]{1,0:T(8,128)} %add.293.mine_ref), channel_id=1, source_target_pairs={{0,4},{4,0},{8,12},{12,8},{16,20},{20,16},{24,28},{28,24},{1,5},{5... | collective-permute-start | bytes 4718600 | tf_op jit(solution)/shard_map/ppermute | solution.py:383
  107.9 3.2 %collective-permute-done.20.refs_15_ = f32[288,512]{1,0:T(8,128)S(1)} collective-permute-done((f32[288,512]{1,0:T(8,128)S(1)}, f32[288,512]{1,0:T(8,128)S(1)}, u32[]{:S(2)}, u32[]{:S(2)}) %collective-permute-start.20) | collective-permute-done | bytes 589856 | tf_op jit(solution)/shard_map/ppermute | solution.py:403
  111.3 2.4 %collective-permute-start.22 = (f32[256,512]{1,0:T(8,128)S(1)}, f32[256,512]{1,0:T(8,128)S(1)}, u32[]{:S(2)}, u32[]{:S(2)}) collective-permute-start(f32[256,512]{1,0:T(8,128)S(1)} %add.295), channel_id=1, source_target_pairs={{0,16},{4,12},{8,24},{12,4},{16,0},{20,28},{24,8},{28,20},{1,17},{... | collective-permute-start | bytes 1572872 | tf_op jit(solution)/shard_map/ppermute | solution.py:393
  113.6 2.1 %collective-permute-start.12 = (f32[296,512]{1,0:T(8,128)}, f32[296,512]{1,0:T(8,128)}, u32[]{:S(2)}, u32[]{:S(2)}) collective-permute-start(f32[296,512]{1,0:T(8,128)} %collective-permute-done.11.refs_11_), channel_id=1, source_target_pairs={{2,1},{6,5},{10,9},{14,13},{18,17},{22,21},{26,25},{30,29}} | collective-permute-start | bytes 1818632 | tf_op jit(solution)/shard_map/ppermute | solution.py:410
  115.7 2.1 %collective-permute-start.13 = (f32[296,512]{1,0:T(8,128)}, f32[296,512]{1,0:T(8,128)}, u32[]{:S(2)}, u32[]{:S(2)}) collective-permute-start(f32[296,512]{1,0:T(8,128)} %collective-permute-done.11.refs_11_), channel_id=1, source_target_pairs={{2,3},{6,7},{10,11},{14,15},{18,19},{22,23},{26,27},{30,31}} | collective-permute-start | bytes 1818632 | tf_op jit(solution)/shard_map/ppermute | solution.py:414
  117.9 2.6 %collective-permute-done.22 = f32[256,512]{1,0:T(8,128)S(1)} collective-permute-done((f32[256,512]{1,0:T(8,128)S(1)}, f32[256,512]{1,0:T(8,128)S(1)}, u32[]{:S(2)}, u32[]{:S(2)}) %collective-permute-start.22) | collective-permute-done | bytes 524320 | tf_op jit(solution)/shard_map/ppermute | solution.py:393
  120.5 0.9 add.296.tm_ref
  121.4 2.1 %collective-permute-start.23 = (f32[256,512]{1,0:T(8,128)}, f32[256,512]{1,0:T(8,128)}, u32[]{:S(2)}, u32[]{:S(2)}) collective-permute-start(f32[256,512]{1,0:T(8,128)} %add.296.tm_ref), channel_id=1, source_target_pairs={{0,4},{4,0},{8,12},{12,8},{16,20},{20,16},{24,28},{28,24},{1,5},{5... | collective-permute-start | bytes 1572872 | tf_op jit(solution)/shard_map/ppermute | solution.py:383
  123.5 0.7 convert_reduce_fusion.4
  124.9 0.6 reduce_max.9
  126.8 2.1 %collective-permute-start.24 = (f32[288,512]{1,0:T(8,128)}, f32[288,512]{1,0:T(8,128)}, u32[]{:S(2)}, u32[]{:S(2)}) collective-permute-start(f32[288,512]{1,0:T(8,128)} %copy-done.12), channel_id=1, source_target_pairs={{2,1},{6,5},{10,9},{14,13},{18,17},{22,21},{26,25},{30,29}} | collective-permute-start | bytes 1769480 | tf_op jit(solution)/shard_map/ppermute | solution.py:410
  128.9 2.1 %collective-permute-start.25 = (f32[288,512]{1,0:T(8,128)}, f32[288,512]{1,0:T(8,128)}, u32[]{:S(2)}, u32[]{:S(2)}) collective-permute-start(f32[288,512]{1,0:T(8,128)} %copy-done.12), channel_id=1, source_target_pairs={{2,3},{6,7},{10,11},{14,15},{18,19},{22,23},{26,27},{30,31}} | collective-permute-start | bytes 1769480 | tf_op jit(solution)/shard_map/ppermute | solution.py:414
  131.0 9.1 %rows.1 = (bf16[1024,1024]{1,0:T(8,128)(2,1)S(1)}, bf16[1024,1024]{1,0:T(8,128)(2,1)S(1)}, f32[512,1024]{1,0:T(8,128)}) custom-call(s32[2]{0:T(128)} %pad_add_fusion.7.where_ref.refs_0_, f32[512,512]{1,0:T(8,128)S(1)} %get-tuple-element.367.panel_ref, f32[256,1536]{1,0:T(8,128)} %add.293.mine_ref, f32[256,1536]{1,0:T(8,128)} %collective-permute-done.16.mate_ref, ...), custom_call_target="tpu_custom_call" | custom-call | flops 10000000000 | bytes 1 | tf_op jit(solution)/shard_map/rows/pallas_call | solution.py:275
  140.2 1.2 collective-permute-done.24.refs_16_
  141.4 2.0 %collective-permute-done.25.refs_17_ = f32[288,512]{1,0:T(8,128)} collective-permute-done((f32[288,512]{1,0:T(8,128)}, f32[288,512]{1,0:T(8,128)}, u32[]{:S(2)}, u32[]{:S(2)}) %collective-permute-start.25) | collective-permute-done | bytes 589856 | tf_op jit(solution)/shard_map/ppermute | solution.py:414
  143.4 8.2 %finish.1 = f32[512,1024]{1,0:T(8,128)} custom-call(s32[2]{0:T(128)} %pad_add_fusion.7.where_ref.refs_0_, s32[72]{0:T(128)} %get-tuple-element.386.target_ref.refs_1_, s32[1]{0:T(128)} %bitcast.18.count_ref.refs_2_, f32[512,1024]{1,0:T(8,128)} %get-tuple-element.364.refs_3_, bf16[1024,1024]{1,0:T(8,128)(2,1)S(1)} %get-tuple-element.668.refs_4_, ...), custom_call_target="tpu_custom_call" | custom-call | flops 10000000000 | bytes 1 | tf_op jit(solution)/shard_map/finish/pallas_call | solution.py:343
  (85 shorter events, 7.8 us)
Async XLA Ops:
  0.0 10.6 %copy-start = (f32[512,1024]{1,0:T(8,128)S(1)}, f32[512,1024]{1,0:T(8,128)}, u32[]{:S(2)}) copy-start(f32[512,1024]{1,0:T(8,128)} %refs_2_.3) | copy-start | bytes 6291460
  0.0 4.6 %copy-start.10 = (s32[2,512]{1,0:T(2,128)S(1)}, s32[2,512]{1,0:T(2,128)}, u32[]{:S(2)}) copy-start(s32[2,512]{1,0:T(2,128)} %param.7) | copy-start | bytes 12292
  0.0 10.6 %collective-permute-start.6 = (f32[512,1024]{1,0:T(8,128)}, f32[512,1024]{1,0:T(8,128)}, u32[]{:S(2)}, u32[]{:S(2)}) collective-permute-start(f32[512,1024]{1,0:T(8,128)} %refs_2_.3), channel_id=1, source_target_pairs={{0,4},{4,0},{8,12},{12,8},{16,20},{20,16},{24,28},{28,24},{1,5},{5... | collective-permute-start | bytes 6291464 | tf_op jit(solution)/shard_map/ppermute | solution.py:383
  3.2 13.2 %copy-start.9 = (f32[512,512]{1,0:T(8,128)}, f32[512,512]{1,0:T(8,128)S(1)}, u32[]{:S(2)}) copy-start(f32[512,512]{1,0:T(8,128)S(1)} %fusion.40.one_ref.refs_2_.refs_6_) | copy-start | bytes 3145732
  3.2 27.5 %collective-permute-start.7 = (f32[512,512]{1,0:T(8,128)S(1)}, f32[512,512]{1,0:T(8,128)}, u32[]{:S(2)}, u32[]{:S(2)}) collective-permute-start(f32[512,512]{1,0:T(8,128)S(1)} %fusion.40.one_ref.refs_2_.refs_6_), channel_id=1, source_target_pairs={{0,2},{4,6},{8,10},{12,14},{16,18},{20,22},{24,26},{28,30}} | collective-permute-start | bytes 3145736 | tf_op jit(solution)/shard_map/ppermute | solution.py:403
  16.4 17.5 %copy-start.6 = (f32[560,512]{1,0:T(8,128)S(1)}, f32[560,512]{1,0:T(8,128)}, u32[]{:S(2)}) copy-start(f32[560,512]{1,0:T(8,128)} %pick.7) | copy-start | bytes 3440644
  16.4 17.5 %collective-permute-start.8 = (f32[560,512]{1,0:T(8,128)}, f32[560,512]{1,0:T(8,128)S(1)}, u32[]{:S(2)}, u32[]{:S(2)}) collective-permute-start(f32[560,512]{1,0:T(8,128)} %pick.7), channel_id=1, source_target_pairs={{0,8},{4,20},{8,0},{12,28},{16,24},{20,4},{24,16},{28,12},{1,9},{5... | collective-permute-start | bytes 3440648 | tf_op jit(solution)/shard_map/ppermute | solution.py:393
  34.1 15.1 %collective-permute-start.9 = (f32[560,512]{1,0:T(8,128)S(1)}, f32[560,512]{1,0:T(8,128)S(1)}, u32[]{:S(2)}, u32[]{:S(2)}) collective-permute-start(f32[560,512]{1,0:T(8,128)S(1)} %add.289), channel_id=1, source_target_pairs={{0,16},{4,12},{8,24},{12,4},{16,0},{20,28},{24,8},{28,20},{1,17},{... | collective-permute-start | bytes 3440648 | tf_op jit(solution)/shard_map/ppermute | solution.py:393
  49.4 8.1 %copy-start.8 = (f32[560,512]{1,0:T(8,128)}, f32[560,512]{1,0:T(8,128)S(1)}, u32[]{:S(2)}) copy-start(f32[560,512]{1,0:T(8,128)S(1)} %add.290.mine_ref) | copy-start | bytes 3440644
  49.4 16.4 %collective-permute-start.10 = (f32[560,512]{1,0:T(8,128)S(1)}, f32[560,512]{1,0:T(8,128)}, u32[]{:S(2)}, u32[]{:S(2)}) collective-permute-start(f32[560,512]{1,0:T(8,128)S(1)} %add.290.mine_ref), channel_id=1, source_target_pairs={{0,4},{4,0},{8,12},{12,8},{16,20},{20,16},{24,28},{28,24},{1,5},{5... | collective-permute-start | bytes 3440648 | tf_op jit(solution)/shard_map/ppermute | solution.py:383
  57.5 19.9 %collective-permute-start.14 = (f32[256,1536]{1,0:T(8,128)}, f32[256,1536]{1,0:T(8,128)}, u32[]{:S(2)}, u32[]{:S(2)}) collective-permute-start(f32[256,1536]{1,0:T(8,128)} %pick.8), channel_id=1, source_target_pairs={{0,8},{4,20},{8,0},{12,28},{16,24},{20,4},{24,16},{28,12},{1,9},{5... | collective-permute-start | bytes 4718600 | tf_op jit(solution)/shard_map/ppermute | solution.py:393
  61.3 24.1 %collective-permute-start.17 = (f32[512,512]{1,0:T(8,128)}, f32[512,512]{1,0:T(8,128)}, u32[]{:S(2)}, u32[]{:S(2)}) collective-permute-start(f32[512,512]{1,0:T(8,128)} %collective-permute-done.7.refs_3_.refs_7_), channel_id=1, source_target_pairs={{2,1},{6,5},{10,9},{14,13},{18,17},{22,21},{26,25},{30,29}} | collective-permute-start | bytes 3145736 | tf_op jit(solution)/shard_map/ppermute | solution.py:410
  63.6 24.1 %collective-permute-start.18 = (f32[512,512]{1,0:T(8,128)}, f32[512,512]{1,0:T(8,128)}, u32[]{:S(2)}, u32[]{:S(2)}) collective-permute-start(f32[512,512]{1,0:T(8,128)} %collective-permute-done.7.refs_3_.refs_7_), channel_id=1, source_target_pairs={{2,3},{6,7},{10,11},{14,15},{18,19},{22,23},{26,27},{30,31}} | collective-permute-start | bytes 3145736 | tf_op jit(solution)/shard_map/ppermute | solution.py:414
  65.8 11.6 %copy-start.7 = (f32[256,1536]{1,0:T(8,128)S(1)}, f32[256,1536]{1,0:T(8,128)}, u32[]{:S(2)}) copy-start(f32[256,1536]{1,0:T(8,128)} %pick.8) | copy-start | bytes 4718596
  80.2 20.6 %collective-permute-start.15 = (f32[256,1536]{1,0:T(8,128)}, f32[256,1536]{1,0:T(8,128)}, u32[]{:S(2)}, u32[]{:S(2)}) collective-permute-start(f32[256,1536]{1,0:T(8,128)} %add.292), channel_id=1, source_target_pairs={{0,16},{4,12},{8,24},{12,4},{16,0},{20,28},{24,8},{28,20},{1,17},{... | collective-permute-start | bytes 4718600 | tf_op jit(solution)/shard_map/ppermute | solution.py:393
  81.4 11.4 %copy-start.11 = (f32[288,512]{1,0:T(8,128)S(1)}, f32[288,512]{1,0:T(8,128)}, u32[]{:S(2)}) copy-start(f32[288,512]{1,0:T(8,128)} %get-tuple-element.376.refs_14_) | copy-start | bytes 1769476
  81.4 17.3 %collective-permute-start.11 = (f32[296,512]{1,0:T(8,128)}, f32[296,512]{1,0:T(8,128)}, u32[]{:S(2)}, u32[]{:S(2)}) collective-permute-start(f32[296,512]{1,0:T(8,128)} %get-tuple-element.366.refs_10_), channel_id=1, source_target_pairs={{0,2},{4,6},{8,10},{12,14},{16,18},{20,22},{24,26},{28,30}} | collective-permute-start | bytes 1818632 | tf_op jit(solution)/shard_map/ppermute | solution.py:403
  91.8 2.6 %collective-permute-start.19 = (f32[256,512]{1,0:T(8,128)}, f32[256,512]{1,0:T(8,128)S(1)}, u32[]{:S(2)}, u32[]{:S(2)}) collective-permute-start(f32[256,512]{1,0:T(8,128)} %get-tuple-element.375), channel_id=1, source_target_pairs={{0,4},{4,0},{8,12},{12,8},{16,20},{20,16},{24,28},{28,24},{1,5},{5... | collective-permute-start | bytes 1572872 | tf_op jit(solution)/shard_map/ppermute | solution.py:383
  92.7 18.5 %collective-permute-start.20 = (f32[288,512]{1,0:T(8,128)S(1)}, f32[288,512]{1,0:T(8,128)S(1)}, u32[]{:S(2)}, u32[]{:S(2)}) collective-permute-start(f32[288,512]{1,0:T(8,128)S(1)} %copy-done.11), channel_id=1, source_target_pairs={{0,2},{4,6},{8,10},{12,14},{16,18},{20,22},{24,26},{28,30}} | collective-permute-start | bytes 1769480 | tf_op jit(solution)/shard_map/ppermute | solution.py:403
  95.6 15.6 %collective-permute-start.21 = (f32[256,512]{1,0:T(8,128)S(1)}, f32[256,512]{1,0:T(8,128)S(1)}, u32[]{:S(2)}, u32[]{:S(2)}) collective-permute-start(f32[256,512]{1,0:T(8,128)S(1)} %add.294), channel_id=1, source_target_pairs={{0,8},{4,20},{8,0},{12,28},{16,24},{20,4},{24,16},{28,12},{1,9},{5... | collective-permute-start | bytes 1572872 | tf_op jit(solution)/shard_map/ppermute | solution.py:393
  104.1 27.0 %collective-permute-start.16 = (f32[256,1536]{1,0:T(8,128)}, f32[256,1536]{1,0:T(8,128)}, u32[]{:S(2)}, u32[]{:S(2)}) collective-permute-start(f32[256,1536]{1,0:T(8,128)} %add.293.mine_ref), channel_id=1, source_target_pairs={{0,4},{4,0},{8,12},{12,8},{16,20},{20,16},{24,28},{28,24},{1,5},{5... | collective-permute-start | bytes 4718600 | tf_op jit(solution)/shard_map/ppermute | solution.py:383
  111.2 10.2 %copy-start.12 = (f32[288,512]{1,0:T(8,128)}, f32[288,512]{1,0:T(8,128)S(1)}, u32[]{:S(2)}) copy-start(f32[288,512]{1,0:T(8,128)S(1)} %collective-permute-done.20.refs_15_) | copy-start | bytes 1769476
  111.3 9.2 %collective-permute-start.22 = (f32[256,512]{1,0:T(8,128)S(1)}, f32[256,512]{1,0:T(8,128)S(1)}, u32[]{:S(2)}, u32[]{:S(2)}) collective-permute-start(f32[256,512]{1,0:T(8,128)S(1)} %add.295), channel_id=1, source_target_pairs={{0,16},{4,12},{8,24},{12,4},{16,0},{20,28},{24,8},{28,20},{1,17},{... | collective-permute-start | bytes 1572872 | tf_op jit(solution)/shard_map/ppermute | solution.py:393
  113.6 15.3 %collective-permute-start.12 = (f32[296,512]{1,0:T(8,128)}, f32[296,512]{1,0:T(8,128)}, u32[]{:S(2)}, u32[]{:S(2)}) collective-permute-start(f32[296,512]{1,0:T(8,128)} %collective-permute-done.11.refs_11_), channel_id=1, source_target_pairs={{2,1},{6,5},{10,9},{14,13},{18,17},{22,21},{26,25},{30,29}} | collective-permute-start | bytes 1818632 | tf_op jit(solution)/shard_map/ppermute | solution.py:410
  115.7 15.3 %collective-permute-start.13 = (f32[296,512]{1,0:T(8,128)}, f32[296,512]{1,0:T(8,128)}, u32[]{:S(2)}, u32[]{:S(2)}) collective-permute-start(f32[296,512]{1,0:T(8,128)} %collective-permute-done.11.refs_11_), channel_id=1, source_target_pairs={{2,3},{6,7},{10,11},{14,15},{18,19},{22,23},{26,27},{30,31}} | collective-permute-start | bytes 1818632 | tf_op jit(solution)/shard_map/ppermute | solution.py:414
  121.4 9.6 %collective-permute-start.23 = (f32[256,512]{1,0:T(8,128)}, f32[256,512]{1,0:T(8,128)}, u32[]{:S(2)}, u32[]{:S(2)}) collective-permute-start(f32[256,512]{1,0:T(8,128)} %add.296.tm_ref), channel_id=1, source_target_pairs={{0,4},{4,0},{8,12},{12,8},{16,20},{20,16},{24,28},{28,24},{1,5},{5... | collective-permute-start | bytes 1572872 | tf_op jit(solution)/shard_map/ppermute | solution.py:383
  126.8 14.6 %collective-permute-start.24 = (f32[288,512]{1,0:T(8,128)}, f32[288,512]{1,0:T(8,128)}, u32[]{:S(2)}, u32[]{:S(2)}) collective-permute-start(f32[288,512]{1,0:T(8,128)} %copy-done.12), channel_id=1, source_target_pairs={{2,1},{6,5},{10,9},{14,13},{18,17},{22,21},{26,25},{30,29}} | collective-permute-start | bytes 1769480 | tf_op jit(solution)/shard_map/ppermute | solution.py:410
  128.9 14.5 %collective-permute-start.25 = (f32[288,512]{1,0:T(8,128)}, f32[288,512]{1,0:T(8,128)}, u32[]{:S(2)}, u32[]{:S(2)}) collective-permute-start(f32[288,512]{1,0:T(8,128)} %copy-done.12), channel_id=1, source_target_pairs={{2,3},{6,7},{10,11},{14,15},{18,19},{22,23},{26,27},{30,31}} | collective-permute-start | bytes 1769480 | tf_op jit(solution)/shard_map/ppermute | solution.py:414
  140.2 11.4 %copy-start.2 = (bf16[1024,1024]{1,0:T(8,128)(2,1)}, bf16[1024,1024]{1,0:T(8,128)(2,1)S(1)}, u32[]{:S(2)}) copy-start(bf16[1024,1024]{1,0:T(8,128)(2,1)S(1)} %get-tuple-element.668.refs_4_) | copy-start | bytes 6291460
  140.2 11.4 %copy-start.3 = (bf16[1024,1024]{1,0:T(8,128)(2,1)}, bf16[1024,1024]{1,0:T(8,128)(2,1)S(1)}, u32[]{:S(2)}) copy-start(bf16[1024,1024]{1,0:T(8,128)(2,1)S(1)} %get-tuple-element.669.refs_5_) | copy-start | bytes 6291460
